TPU v7x, 32 devices: a whole 2x2x4 slice. The times are simulated.
32 devices in a mesh: gx: 4 (over y, x), gy: 8 (over z, core).
Axes of the slice: x: 2, y: 2, z: 4, core: 2. Of those that a mesh axis runs over, the one named last changes fastest.
Arguments:
- velocity: float32 [3, 32, 128, 256], P(None, 'gx', 'gy'), may hold values from -6 to 6
- pressure: float32 [32, 128, 256], P('gx', 'gy'), may hold values from -4 to 4
- part_cell: int32 [4, 8, 8, 512], P('gx', 'gy'), may hold values from 0 to 32767
- part_count: int32 [4, 8, 8], P('gx', 'gy'), may hold values from 1 to 512, as said below
- grain_velocities: float32 [4, 8, 8, 3, 512], P('gx', 'gy'), may hold values from -6 to 6
- part_vol: float32 [4, 8, 8, 512], P('gx', 'gy'), may hold values from 0.05 to 0.3
Outputs:
- velocity_out: float32 [3, 32, 128, 256], P(None, 'gx', 'gy')
- pressure_out: float32 [32, 128, 256], P('gx', 'gy')
- drag: float32 [4, 8, 8, 3, 512], P('gx', 'gy')
Inputs may be any that keep to these rules, and one draw needn't show every extreme that they name: Every DEM owner (a, b) has at least one c with part_count[a, b, c] equal to 512.
All inputs are finite; a program needn't handle non-finite values.
Results may differ from a plain program's by a relative error of at most 0.00002.
Values sent between devices are 32-bit elements; how exact they have to be, the bound alone decides.
A program may use at most 128 MiB of HBM per device.

v0:
```python
import jax
import jax.numpy as jnp
from jax import lax
from jax.sharding import PartitionSpec as P

STEPS = 2
SWEEPS = 4


drag_coefficient = 2.0
time_step = 0.25
viscosity = 0.2
eps_floor = 0.4


def extended(block, sides, width):
    for axis, dim in sides:
        count = lax.axis_size(axis)
        forward = [(i, i + 1) for i in range(count - 1)]
        backward = [(target, source) for source, target in forward]
        low = lax.ppermute(
            lax.slice_in_dim(block, block.shape[dim] - width, None, axis=dim), axis, forward
        )
        high = lax.ppermute(lax.slice_in_dim(block, 0, width, axis=dim), axis, backward)
        block = jnp.concatenate([low, block, high], axis=dim)
    return block


def cell_faces(padded):
    return [
        padded[..., 2:, 1:-1, 1:-1],
        padded[..., :-2, 1:-1, 1:-1],
        padded[..., 1:-1, 2:, 1:-1],
        padded[..., 1:-1, :-2, 1:-1],
        padded[..., 1:-1, 1:-1, 2:],
        padded[..., 1:-1, 1:-1, :-2],
    ]


def padding_thickness(field):
    widths = [(0, 0)] * (field.ndim - 1) + [(1, 1)]
    return jnp.pad(field, widths)


def laplacian_operator(padded_velocity_field, flow_velocity, padded_voidage, porous_medium):
    near = cell_faces(padded_velocity_field)
    kernel_weights = cell_faces(padded_voidage)
    total = jnp.zeros_like(flow_velocity)
    for index in range(6):
        total = (
            total
            + 0.5
            * (porous_medium + kernel_weights[index])
            * (near[index] - flow_velocity)
            / porous_medium
        )
    return total


def divergence(flux_pad):
    near = cell_faces(flux_pad)
    return (
        0.5
        / time_step
        * (near[0][0] - near[1][0] + (near[2][1] - near[3][1]) + (near[4][2] - near[5][2]))
    )


def relaxation_terms(padded_pressure_field, padded_voidage):
    central_value = padded_voidage[1:-1, 1:-1, 1:-1]
    near = cell_faces(padded_pressure_field)
    kernel_weights = cell_faces(padded_voidage)
    numerator = jnp.zeros_like(central_value)
    denominator = jnp.zeros_like(central_value)
    for index in range(6):
        weight = 0.5 * (central_value + kernel_weights[index])
        numerator = numerator + weight * near[index]
        denominator = denominator + weight
    return (numerator, denominator)


def gradient(padded_pressure_field):
    near = cell_faces(padded_pressure_field)
    return jnp.stack(
        [0.5 * (near[0] - near[1]), 0.5 * (near[2] - near[3]), 0.5 * (near[4] - near[5])]
    )


def per_device(velocity, pressure, part_cell, part_count, grain_velocities, part_vol):
    rows_x, rows_y, depth = pressure.shape
    capacity = part_vol.shape[-1]
    grid_cells = rows_x * rows_y * depth
    slots = jnp.arange(capacity, dtype=jnp.int32)
    alive = slots[None, None, None, :] < part_count[..., None]
    grain_volume = jnp.where(alive, part_vol, jnp.float32(0.0))
    loads = jnp.concatenate([grain_velocities, grain_volume[..., None, :]], axis=3)
    got_cell = lax.all_to_all(part_cell, "gy", split_axis=2, concat_axis=2, tiled=True)
    got_load = lax.all_to_all(loads, "gy", split_axis=2, concat_axis=2, tiled=True)
    target_field = got_cell.reshape(-1)
    got_vol = got_load[..., 3, :]
    got_vel = got_load[..., :3, :]
    carried = jnp.moveaxis(got_vol[..., None, :] * got_vel, 3, 4).reshape(-1, 3)
    solid = jax.ops.segment_sum(got_vol.reshape(-1), target_field, num_segments=grid_cells).reshape(
        rows_x, rows_y, depth
    )
    mass_flux = jax.ops.segment_sum(carried, target_field, num_segments=grid_cells).T.reshape(
        3, rows_x, rows_y, depth
    )
    porous_medium = jnp.maximum(1.0 - solid, eps_floor)
    widened_field = extended(porous_medium, (("gx", 0), ("gy", 1)), 2)
    padded_voidage = padding_thickness(widened_field[1:-1, 1:-1])
    for step in range(STEPS):
        velocity_rotation = extended(velocity, (("gx", 1), ("gy", 2)), 1)
        spread_to_mesh = laplacian_operator(
            padding_thickness(velocity_rotation), velocity, padded_voidage, porous_medium
        )
        force = drag_coefficient * (mass_flux - solid * velocity) / porous_medium
        guess = velocity + time_step * (viscosity * spread_to_mesh + force)
        flux_cycle = extended(porous_medium * guess, (("gx", 1), ("gy", 2)), 1)
        source = divergence(padding_thickness(flux_cycle))
        for sweep in range(SWEEPS):
            pressure_rotation = extended(pressure, (("gx", 0), ("gy", 1)), 1)
            numerator, denominator = relaxation_terms(
                padding_thickness(pressure_rotation), padded_voidage
            )
            pressure = (numerator - source) / denominator
        slope_cycle = extended(pressure, (("gx", 0), ("gy", 1)), 1)
        velocity = guess - time_step * gradient(padding_thickness(slope_cycle))
    flat_vel = velocity.reshape(3, grid_cells)
    flattened_voids = porous_medium.reshape(grid_cells)
    slot_shape_factors = got_vol.shape
    cell_flow_speed = jnp.moveaxis(
        flat_vel[:, target_field].reshape((3,) + slot_shape_factors), 0, 3
    )
    cell_void_fraction = flattened_voids[target_field].reshape(slot_shape_factors)
    coupled_state = jnp.concatenate([cell_flow_speed, cell_void_fraction[..., None, :]], axis=3)
    back = lax.all_to_all(coupled_state, "gy", split_axis=2, concat_axis=2, tiled=True)
    drag = (
        grain_volume[..., None, :]
        * drag_coefficient
        * (back[..., :3, :] - grain_velocities)
        / back[..., 3:4, :]
    )
    return (velocity, pressure, drag)


def solution(mesh):
    placed = (
        P(None, "gx", "gy", None),
        P("gx", "gy", None),
        P("gx", "gy", None, None),
        P("gx", "gy", None),
        P("gx", "gy", None, None, None),
        P("gx", "gy", None, None),
    )
    return jax.shard_map(
        per_device,
        mesh=mesh,
        in_specs=placed,
        out_specs=(P(None, "gx", "gy", None), P("gx", "gy", None), P("gx", "gy", None, None, None)),
        check_vma=False,
    )
```

profile of v0, /device:TPU:0, one launch (start us, length us, event | category | flops | bytes accessed | tf_op | source)
XLA Modules:
  0.0 357.2 jit_solution(8799463692055073704)
XLA Ops:
  3.6 6.4 %all-to-all-start.1 = ((f32[1,1,8,4,512]{4,3,1,0,2:T(4,128)}), f32[1,1,8,4,512]{4,3,1,0,2:T(4,128)S(1)}, u32[]{:S(2)}, u32[]{:S(2)}) async-start(f32[1,1,8,4,512]{4,3,1,0,2:T(4,128)} %pad_maximum_fusion.104), calls=%async_computation.1 | async-start | bytes 131072 | tf_op jit(solution)/shard_map/all_to_all | solution.py:98
  10.7 3.4 collective-permute-start.9
  14.9 3.4 collective-permute-start.3
  23.2 2.7 collective-permute-done.8
  26.0 5.1 %all-to-all-start = ((s32[1,1,8,512]{3,1,0,2:T(1,128)}), s32[1,1,8,512]{3,1,0,2:T(1,128)S(1)}, u32[]{:S(2)}, u32[]{:S(2)}) async-start(s32[1,1,8,512]{3,1,0,2:T(1,128)} %copy.25), calls=%async_computation | async-start | bytes 32768 | tf_op jit(solution)/shard_map/all_to_all | solution.py:97
  32.5 3.0 collective-permute-start.7
  36.8 21.9 %scatter_custom_fusion = f32[32768]{0:T(1024)S(1)} fusion(s32[4096]{0:T(1024)S(1)} %bitcast.52, f32[4096]{0:T(1024)S(1)} %bitcast.56, f32[]{:T(128)} %constant.10.clone.1), kind=kCustom, calls=%fused_computation.368 | custom fusion | flops 4096 | bytes 131076 | tf_op jit(solution)/shard_map/scatter-add | solution.py:103
  60.8 5.4 %collective-permute-start.2 = (f32[2,16,256]{2,1,0:T(8,128)S(1)}, f32[2,16,256]{2,1,0:T(8,128)S(1)}, u32[]{:S(2)}, u32[]{:S(2)}) collective-permute-start(f32[2,16,256]{2,1,0:T(8,128)S(1)} %get-tuple-element.83), channel_id=1, source_target_pairs={{0,8},{8,16},{16,24},{1,9},{9,17},{17,25},{2,10},{10,18},{18,26},{... | collective-permute-start | bytes 98312 | tf_op jit(solution)/shard_map/ppermute | solution.py:21
  69.1 3.0 collective-permute-start.6
  72.2 2.0 copy.29
  74.2 29.5 %scatter_custom_fusion.1 = f32[32768,3]{1,0:T(8,128)} fusion(s32[4096]{0:T(1024)S(1)} %bitcast.53, f32[4096,3]{1,0:T(8,128)} %copy.29, f32[]{:T(128)} %constant.10.clone.1), kind=kCustom, calls=%fused_computation.4 | custom fusion | flops 12288 | bytes 393728 | tf_op jit(solution)/shard_map/scatter-add | solution.py:106
  103.7 10.0 %copy.30 = f32[3,8,16,256]{3,2,1,0:T(8,128)S(1)} copy(f32[3,8,16,256]{0,3,2,1:T(8,128)} %bitcast.45) | data formatting | bytes 786432 | tf_op jit(solution)/shard_map/reshape | solution.py:106
  118.0 5.4 %collective-permute-start.13 = (f32[3,1,16,256]{3,2,1,0:T(8,128)S(1)}, f32[3,1,16,256]{3,2,1,0:T(8,128)S(1)}, u32[]{:S(2)}, u32[]{:S(2)}) collective-permute-start(f32[3,1,16,256]{3,2,1,0:T(8,128)S(1)} %get-tuple-element.33), channel_id=1, source_target_pairs={{0,8},{8,16},{16,24},{1,9},{9,17},{17,25},{2,10},{10,18},{18,26},{... | collective-permute-start | bytes 147464 | tf_op jit(solution)/shard_map/ppermute | solution.py:21
  124.8 3.0 collective-permute-start.11
  129.2 4.3 %collective-permute-start.15 = (f32[3,10,1,256]{3,2,1,0:T(1,128)S(1)}, f32[3,10,1,256]{3,2,1,0:T(1,128)S(1)}, u32[]{:S(2)}, u32[]{:S(2)}) collective-permute-start(f32[3,10,1,256]{3,2,1,0:T(1,128)S(1)} %get-tuple-element.25), channel_id=1, source_target_pairs={{0,1},{1,2},{2,3},{3,4},{4,5},{5,6},{6,7},{8,9},{9,10},{10,11},{11... | collective-permute-start | bytes 92168 | tf_op jit(solution)/shard_map/ppermute | solution.py:21
  136.6 5.8 %collective-permute-start.17 = (f32[1,16,256]{2,1,0:T(8,128)S(1)}, f32[1,16,256]{2,1,0:T(8,128)S(1)}, u32[]{:S(2)}, u32[]{:S(2)}) collective-permute-start(f32[1,16,256]{2,1,0:T(8,128)S(1)} %get-tuple-element.79), channel_id=1, source_target_pairs={{0,8},{8,16},{16,24},{1,9},{9,17},{17,25},{2,10},{10,18},{18,26},{... | collective-permute-start | bytes 49160 | tf_op jit(solution)/shard_map/ppermute | solution.py:21
  142.4 1.4 collective-permute-done.17
  145.2 3.6 collective-permute-start.19
  151.3 5.2 %collective-permute-start.21 = (f32[1,16,256]{2,1,0:T(8,128)S(1)}, f32[1,16,256]{2,1,0:T(8,128)S(1)}, u32[]{:S(2)}, u32[]{:S(2)}) collective-permute-start(f32[1,16,256]{2,1,0:T(8,128)S(1)} %get-tuple-element.77), channel_id=1, source_target_pairs={{0,8},{8,16},{16,24},{1,9},{9,17},{17,25},{2,10},{10,18},{18,26},{... | collective-permute-start | bytes 49160 | tf_op jit(solution)/shard_map/ppermute | solution.py:21
  156.4 1.4 collective-permute-done.21
  159.2 5.3 %collective-permute-start.23 = (f32[10,1,256]{2,1,0:T(1,128)S(1)}, f32[10,1,256]{2,1,0:T(1,128)S(1)}, u32[]{:S(2)}, u32[]{:S(2)}) collective-permute-start(f32[10,1,256]{2,1,0:T(1,128)S(1)} %get-tuple-element.57), channel_id=1, source_target_pairs={{0,1},{1,2},{2,3},{3,4},{4,5},{5,6},{6,7},{8,9},{9,10},{10,11},{11... | collective-permute-start | bytes 30728 | tf_op jit(solution)/shard_map/ppermute | solution.py:21
  166.8 5.7 %collective-permute-start.25 = (f32[1,16,256]{2,1,0:T(8,128)S(1)}, f32[1,16,256]{2,1,0:T(8,128)S(1)}, u32[]{:S(2)}, u32[]{:S(2)}) collective-permute-start(f32[1,16,256]{2,1,0:T(8,128)S(1)} %get-tuple-element.75), channel_id=1, source_target_pairs={{0,8},{8,16},{16,24},{1,9},{9,17},{17,25},{2,10},{10,18},{18,26},{... | collective-permute-start | bytes 49160 | tf_op jit(solution)/shard_map/ppermute | solution.py:21
  172.6 1.4 collective-permute-done.25
  175.3 4.8 %collective-permute-start.27 = (f32[10,1,256]{2,1,0:T(1,128)S(1)}, f32[10,1,256]{2,1,0:T(1,128)S(1)}, u32[]{:S(2)}, u32[]{:S(2)}) collective-permute-start(f32[10,1,256]{2,1,0:T(1,128)S(1)} %get-tuple-element.55), channel_id=1, source_target_pairs={{0,1},{1,2},{2,3},{3,4},{4,5},{5,6},{6,7},{8,9},{9,10},{10,11},{11... | collective-permute-start | bytes 30728 | tf_op jit(solution)/shard_map/ppermute | solution.py:21
  182.6 5.7 %collective-permute-start.29 = (f32[1,16,256]{2,1,0:T(8,128)S(1)}, f32[1,16,256]{2,1,0:T(8,128)S(1)}, u32[]{:S(2)}, u32[]{:S(2)}) collective-permute-start(f32[1,16,256]{2,1,0:T(8,128)S(1)} %get-tuple-element.73), channel_id=1, source_target_pairs={{0,8},{8,16},{16,24},{1,9},{9,17},{17,25},{2,10},{10,18},{18,26},{... | collective-permute-start | bytes 49160 | tf_op jit(solution)/shard_map/ppermute | solution.py:21
  188.4 1.4 collective-permute-done.29
  191.1 4.8 %collective-permute-start.31 = (f32[10,1,256]{2,1,0:T(1,128)S(1)}, f32[10,1,256]{2,1,0:T(1,128)S(1)}, u32[]{:S(2)}, u32[]{:S(2)}) collective-permute-start(f32[10,1,256]{2,1,0:T(1,128)S(1)} %get-tuple-element.53), channel_id=1, source_target_pairs={{0,1},{1,2},{2,3},{3,4},{4,5},{5,6},{6,7},{8,9},{9,10},{10,11},{11... | collective-permute-start | bytes 30728 | tf_op jit(solution)/shard_map/ppermute | solution.py:21
  198.5 5.7 %collective-permute-start.33 = (f32[3,1,16,256]{3,2,1,0:T(8,128)S(1)}, f32[3,1,16,256]{3,2,1,0:T(8,128)S(1)}, u32[]{:S(2)}, u32[]{:S(2)}) collective-permute-start(f32[3,1,16,256]{3,2,1,0:T(8,128)S(1)} %get-tuple-element.31), channel_id=1, source_target_pairs={{0,8},{8,16},{16,24},{1,9},{9,17},{17,25},{2,10},{10,18},{18,26},{... | collective-permute-start | bytes 147464 | tf_op jit(solution)/shard_map/ppermute | solution.py:21
  204.4 1.6 collective-permute-done.33
  207.4 4.8 %collective-permute-start.35 = (f32[3,10,1,256]{3,2,1,0:T(1,128)S(1)}, f32[3,10,1,256]{3,2,1,0:T(1,128)S(1)}, u32[]{:S(2)}, u32[]{:S(2)}) collective-permute-start(f32[3,10,1,256]{3,2,1,0:T(1,128)S(1)} %get-tuple-element.23), channel_id=1, source_target_pairs={{0,1},{1,2},{2,3},{3,4},{4,5},{5,6},{6,7},{8,9},{9,10},{10,11},{11... | collective-permute-start | bytes 92168 | tf_op jit(solution)/shard_map/ppermute | solution.py:21
  215.5 5.7 %collective-permute-start.37 = (f32[3,1,16,256]{3,2,1,0:T(8,128)S(1)}, f32[3,1,16,256]{3,2,1,0:T(8,128)S(1)}, u32[]{:S(2)}, u32[]{:S(2)}) collective-permute-start(f32[3,1,16,256]{3,2,1,0:T(8,128)S(1)} %get-tuple-element.29), channel_id=1, source_target_pairs={{0,8},{8,16},{16,24},{1,9},{9,17},{17,25},{2,10},{10,18},{18,26},{... | collective-permute-start | bytes 147464 | tf_op jit(solution)/shard_map/ppermute | solution.py:21
  221.4 1.6 collective-permute-done.37
  224.4 5.0 %collective-permute-start.39 = (f32[3,10,1,256]{3,2,1,0:T(1,128)S(1)}, f32[3,10,1,256]{3,2,1,0:T(1,128)S(1)}, u32[]{:S(2)}, u32[]{:S(2)}) collective-permute-start(f32[3,10,1,256]{3,2,1,0:T(1,128)S(1)} %get-tuple-element.21), channel_id=1, source_target_pairs={{0,1},{1,2},{2,3},{3,4},{4,5},{5,6},{6,7},{8,9},{9,10},{10,11},{11... | collective-permute-start | bytes 92168 | tf_op jit(solution)/shard_map/ppermute | solution.py:21
  232.4 5.8 %collective-permute-start.41 = (f32[1,16,256]{2,1,0:T(8,128)S(1)}, f32[1,16,256]{2,1,0:T(8,128)S(1)}, u32[]{:S(2)}, u32[]{:S(2)}) collective-permute-start(f32[1,16,256]{2,1,0:T(8,128)S(1)} %get-tuple-element.71), channel_id=1, source_target_pairs={{0,8},{8,16},{16,24},{1,9},{9,17},{17,25},{2,10},{10,18},{18,26},{... | collective-permute-start | bytes 49160 | tf_op jit(solution)/shard_map/ppermute | solution.py:21
  238.2 1.4 collective-permute-done.41
  240.9 5.0 %collective-permute-start.43 = (f32[10,1,256]{2,1,0:T(1,128)S(1)}, f32[10,1,256]{2,1,0:T(1,128)S(1)}, u32[]{:S(2)}, u32[]{:S(2)}) collective-permute-start(f32[10,1,256]{2,1,0:T(1,128)S(1)} %get-tuple-element.49), channel_id=1, source_target_pairs={{0,1},{1,2},{2,3},{3,4},{4,5},{5,6},{6,7},{8,9},{9,10},{10,11},{11... | collective-permute-start | bytes 30728 | tf_op jit(solution)/shard_map/ppermute | solution.py:21
  248.4 5.8 %collective-permute-start.45 = (f32[1,16,256]{2,1,0:T(8,128)S(1)}, f32[1,16,256]{2,1,0:T(8,128)S(1)}, u32[]{:S(2)}, u32[]{:S(2)}) collective-permute-start(f32[1,16,256]{2,1,0:T(8,128)S(1)} %get-tuple-element.69), channel_id=1, source_target_pairs={{0,8},{8,16},{16,24},{1,9},{9,17},{17,25},{2,10},{10,18},{18,26},{... | collective-permute-start | bytes 49160 | tf_op jit(solution)/shard_map/ppermute | solution.py:21
  254.2 1.4 collective-permute-done.45
  257.0 4.8 %collective-permute-start.47 = (f32[10,1,256]{2,1,0:T(1,128)S(1)}, f32[10,1,256]{2,1,0:T(1,128)S(1)}, u32[]{:S(2)}, u32[]{:S(2)}) collective-permute-start(f32[10,1,256]{2,1,0:T(1,128)S(1)} %get-tuple-element.47), channel_id=1, source_target_pairs={{0,1},{1,2},{2,3},{3,4},{4,5},{5,6},{6,7},{8,9},{9,10},{10,11},{11... | collective-permute-start | bytes 30728 | tf_op jit(solution)/shard_map/ppermute | solution.py:21
  264.3 5.7 %collective-permute-start.49 = (f32[1,16,256]{2,1,0:T(8,128)S(1)}, f32[1,16,256]{2,1,0:T(8,128)S(1)}, u32[]{:S(2)}, u32[]{:S(2)}) collective-permute-start(f32[1,16,256]{2,1,0:T(8,128)S(1)} %get-tuple-element.67), channel_id=1, source_target_pairs={{0,8},{8,16},{16,24},{1,9},{9,17},{17,25},{2,10},{10,18},{18,26},{... | collective-permute-start | bytes 49160 | tf_op jit(solution)/shard_map/ppermute | solution.py:21
  272.8 4.8 %collective-permute-start.51 = (f32[10,1,256]{2,1,0:T(1,128)S(1)}, f32[10,1,256]{2,1,0:T(1,128)S(1)}, u32[]{:S(2)}, u32[]{:S(2)}) collective-permute-start(f32[10,1,256]{2,1,0:T(1,128)S(1)} %get-tuple-element.45), channel_id=1, source_target_pairs={{0,1},{1,2},{2,3},{3,4},{4,5},{5,6},{6,7},{8,9},{9,10},{10,11},{11... | collective-permute-start | bytes 30728 | tf_op jit(solution)/shard_map/ppermute | solution.py:21
  280.2 5.7 %collective-permute-start.53 = (f32[1,16,256]{2,1,0:T(8,128)S(1)}, f32[1,16,256]{2,1,0:T(8,128)S(1)}, u32[]{:S(2)}, u32[]{:S(2)}) collective-permute-start(f32[1,16,256]{2,1,0:T(8,128)S(1)} %get-tuple-element.65), channel_id=1, source_target_pairs={{0,8},{8,16},{16,24},{1,9},{9,17},{17,25},{2,10},{10,18},{18,26},{... | collective-permute-start | bytes 49160 | tf_op jit(solution)/shard_map/ppermute | solution.py:21
  288.6 4.8 %collective-permute-start.55 = (f32[10,1,256]{2,1,0:T(1,128)S(1)}, f32[10,1,256]{2,1,0:T(1,128)S(1)}, u32[]{:S(2)}, u32[]{:S(2)}) collective-permute-start(f32[10,1,256]{2,1,0:T(1,128)S(1)} %get-tuple-element.43), channel_id=1, source_target_pairs={{0,1},{1,2},{2,3},{3,4},{4,5},{5,6},{6,7},{8,9},{9,10},{10,11},{11... | collective-permute-start | bytes 30728 | tf_op jit(solution)/shard_map/ppermute | solution.py:21
  293.5 23.0 %gather_fusion.1 = f32[4096]{0:T(1024)S(1)} fusion(f32[32768]{0:T(1024)S(1)} %subtract_maximum_fusion, s32[4096]{0:T(1024)S(1)} %broadcast_clamp_fusion), kind=kCustom, calls=%fused_computation.1 | custom fusion | bytes 49152 | tf_op jit(solution)/shard_map/gather | solution.py:135
  317.0 8.7 %copy.32 = f32[3,8,16,256]{0,3,2,1:T(8,128)} copy(f32[3,8,16,256]{3,2,1,0:T(8,128)S(1)} %fusion.54) | data formatting | bytes 786432 | tf_op jit(solution)/shard_map/sub | solution.py:128
  325.8 16.5 %gather_fusion = f32[4096,3]{1,0:T(8,128)S(1)} fusion(f32[3,32768]{0,1:T(8,128)} %bitcast.46, s32[4096]{0:T(1024)S(1)} %broadcast_clamp_fusion), kind=kCustom, calls=%fused_computation | custom fusion | bytes 114688 | tf_op jit(solution)/shard_map/gather | solution.py:133
  343.7 6.9 %all-to-all-start.2 = ((f32[1,1,8,4,512]{4,3,1,0,2:T(4,128)}), f32[1,1,8,4,512]{4,3,1,0,2:T(4,128)S(1)}, u32[]{:S(2)}, u32[]{:S(2)}) async-start(f32[1,1,8,4,512]{4,3,1,0,2:T(4,128)} %pad_maximum_fusion.105), calls=%async_computation.2 | async-start | bytes 131072 | tf_op jit(solution)/shard_map/all_to_all | solution.py:137
  350.5 5.9 %all-to-all-done.2 = f32[1,1,8,4,512]{4,3,1,0,2:T(4,128)S(1)} async-done(((f32[1,1,8,4,512]{4,3,1,0,2:T(4,128)}), f32[1,1,8,4,512]{4,3,1,0,2:T(4,128)S(1)}, u32[]{:S(2)}, u32[]{:S(2)}) %all-to-all-start.2) | async-done | bytes 65568 | tf_op jit(solution)/shard_map/all_to_all | solution.py:137
  (209 shorter events, 69.2 us)
Async XLA Ops:
  3.6 22.4 %all-to-all-start.1 = ((f32[1,1,8,4,512]{4,3,1,0,2:T(4,128)}), f32[1,1,8,4,512]{4,3,1,0,2:T(4,128)S(1)}, u32[]{:S(2)}, u32[]{:S(2)}) async-start(f32[1,1,8,4,512]{4,3,1,0,2:T(4,128)} %pad_maximum_fusion.104), calls=%async_computation.1 | async-start | bytes 131072 | tf_op jit(solution)/shard_map/all_to_all | solution.py:98
  10.7 11.6 %collective-permute-start.9 = (f32[1,16,256]{2,1,0:T(8,128)S(1)}, f32[1,16,256]{2,1,0:T(8,128)S(1)}, u32[]{:S(2)}, u32[]{:S(2)}) collective-permute-start(f32[1,16,256]{2,1,0:T(8,128)S(1)} %get-tuple-element.82), channel_id=1, source_target_pairs={{0,8},{8,16},{16,24},{1,9},{9,17},{17,25},{2,10},{10,18},{18,26},{... | collective-permute-start | bytes 49160 | tf_op jit(solution)/shard_map/ppermute | solution.py:21
  14.9 11.0 %collective-permute-start.3 = (f32[3,1,16,256]{3,2,1,0:T(8,128)S(1)}, f32[3,1,16,256]{3,2,1,0:T(8,128)S(1)}, u32[]{:S(2)}, u32[]{:S(2)}) collective-permute-start(f32[3,1,16,256]{3,2,1,0:T(8,128)S(1)} %get-tuple-element.36), channel_id=1, source_target_pairs={{0,8},{8,16},{16,24},{1,9},{9,17},{17,25},{2,10},{10,18},{18,26},{... | collective-permute-start | bytes 147464 | tf_op jit(solution)/shard_map/ppermute | solution.py:21
  18.3 7.6 %collective-permute-start.1 = (f32[3,1,16,256]{3,2,1,0:T(8,128)S(1)}, f32[3,1,16,256]{3,2,1,0:T(8,128)S(1)}, u32[]{:S(2)}, u32[]{:S(2)}) collective-permute-start(f32[3,1,16,256]{3,2,1,0:T(8,128)S(1)} %get-tuple-element.35), channel_id=1, source_target_pairs={{8,0},{16,8},{24,16},{9,1},{17,9},{25,17},{10,2},{18,10},{26,18},{... | collective-permute-start | bytes 147464 | tf_op jit(solution)/shard_map/ppermute | solution.py:24
  19.6 6.3 %collective-permute-start.8 = (f32[1,16,256]{2,1,0:T(8,128)S(1)}, f32[1,16,256]{2,1,0:T(8,128)S(1)}, u32[]{:S(2)}, u32[]{:S(2)}) collective-permute-start(f32[1,16,256]{2,1,0:T(8,128)S(1)} %get-tuple-element.81), channel_id=1, source_target_pairs={{8,0},{16,8},{24,16},{9,1},{17,9},{25,17},{10,2},{18,10},{26,18},{... | collective-permute-start | bytes 49160 | tf_op jit(solution)/shard_map/ppermute | solution.py:24
  26.0 10.8 %all-to-all-start = ((s32[1,1,8,512]{3,1,0,2:T(1,128)}), s32[1,1,8,512]{3,1,0,2:T(1,128)S(1)}, u32[]{:S(2)}, u32[]{:S(2)}) async-start(s32[1,1,8,512]{3,1,0,2:T(1,128)} %copy.25), calls=%async_computation | async-start | bytes 32768 | tf_op jit(solution)/shard_map/all_to_all | solution.py:97
  31.2 35.1 %collective-permute-start.5 = (f32[3,10,1,256]{3,2,1,0:T(1,128)S(1)}, f32[3,10,1,256]{3,2,1,0:T(1,128)S(1)}, u32[]{:S(2)}, u32[]{:S(2)}) collective-permute-start(f32[3,10,1,256]{3,2,1,0:T(1,128)S(1)} %get-tuple-element.28), channel_id=1, source_target_pairs={{1,0},{2,1},{3,2},{4,3},{5,4},{6,5},{7,6},{9,8},{10,9},{11,10},{12... | collective-permute-start | bytes 92168 | tf_op jit(solution)/shard_map/ppermute | solution.py:24
  32.5 33.8 %collective-permute-start.7 = (f32[3,10,1,256]{3,2,1,0:T(1,128)S(1)}, f32[3,10,1,256]{3,2,1,0:T(1,128)S(1)}, u32[]{:S(2)}, u32[]{:S(2)}) collective-permute-start(f32[3,10,1,256]{3,2,1,0:T(1,128)S(1)} %get-tuple-element.27), channel_id=1, source_target_pairs={{0,1},{1,2},{2,3},{3,4},{4,5},{5,6},{6,7},{8,9},{9,10},{10,11},{11... | collective-permute-start | bytes 92168 | tf_op jit(solution)/shard_map/ppermute | solution.py:21
  59.5 7.4 %collective-permute-start = (f32[2,16,256]{2,1,0:T(8,128)S(1)}, f32[2,16,256]{2,1,0:T(8,128)S(1)}, u32[]{:S(2)}, u32[]{:S(2)}) collective-permute-start(f32[2,16,256]{2,1,0:T(8,128)S(1)} %get-tuple-element.84), channel_id=1, source_target_pairs={{8,0},{16,8},{24,16},{9,1},{17,9},{25,17},{10,2},{18,10},{26,18},{... | collective-permute-start | bytes 98312 | tf_op jit(solution)/shard_map/ppermute | solution.py:24
  60.8 7.0 %collective-permute-start.2 = (f32[2,16,256]{2,1,0:T(8,128)S(1)}, f32[2,16,256]{2,1,0:T(8,128)S(1)}, u32[]{:S(2)}, u32[]{:S(2)}) collective-permute-start(f32[2,16,256]{2,1,0:T(8,128)S(1)} %get-tuple-element.83), channel_id=1, source_target_pairs={{0,8},{8,16},{16,24},{1,9},{9,17},{17,25},{2,10},{10,18},{18,26},{... | collective-permute-start | bytes 98312 | tf_op jit(solution)/shard_map/ppermute | solution.py:21
  67.8 45.9 %collective-permute-start.4 = (f32[12,2,256]{2,1,0:T(2,128)S(1)}, f32[12,2,256]{2,1,0:T(2,128)S(1)}, u32[]{:S(2)}, u32[]{:S(2)}) collective-permute-start(f32[12,2,256]{2,1,0:T(2,128)S(1)} %get-tuple-element.40), channel_id=1, source_target_pairs={{1,0},{2,1},{3,2},{4,3},{5,4},{6,5},{7,6},{9,8},{10,9},{11,10},{12... | collective-permute-start | bytes 73736 | tf_op jit(solution)/shard_map/ppermute | solution.py:24
  69.1 44.6 %collective-permute-start.6 = (f32[12,2,256]{2,1,0:T(2,128)S(1)}, f32[12,2,256]{2,1,0:T(2,128)S(1)}, u32[]{:S(2)}, u32[]{:S(2)}) collective-permute-start(f32[12,2,256]{2,1,0:T(2,128)S(1)} %get-tuple-element.39), channel_id=1, source_target_pairs={{0,1},{1,2},{2,3},{3,4},{4,5},{5,6},{6,7},{8,9},{9,10},{10,11},{11... | collective-permute-start | bytes 73736 | tf_op jit(solution)/shard_map/ppermute | solution.py:21
  116.7 11.1 %collective-permute-start.12 = (f32[3,1,16,256]{3,2,1,0:T(8,128)S(1)}, f32[3,1,16,256]{3,2,1,0:T(8,128)S(1)}, u32[]{:S(2)}, u32[]{:S(2)}) collective-permute-start(f32[3,1,16,256]{3,2,1,0:T(8,128)S(1)} %get-tuple-element.34), channel_id=1, source_target_pairs={{8,0},{16,8},{24,16},{9,1},{17,9},{25,17},{10,2},{18,10},{26,18},{... | collective-permute-start | bytes 147464 | tf_op jit(solution)/shard_map/ppermute | solution.py:24
  118.0 9.8 %collective-permute-start.13 = (f32[3,1,16,256]{3,2,1,0:T(8,128)S(1)}, f32[3,1,16,256]{3,2,1,0:T(8,128)S(1)}, u32[]{:S(2)}, u32[]{:S(2)}) collective-permute-start(f32[3,1,16,256]{3,2,1,0:T(8,128)S(1)} %get-tuple-element.33), channel_id=1, source_target_pairs={{0,8},{8,16},{16,24},{1,9},{9,17},{17,25},{2,10},{10,18},{18,26},{... | collective-permute-start | bytes 147464 | tf_op jit(solution)/shard_map/ppermute | solution.py:21
  123.5 10.0 %collective-permute-start.10 = (f32[10,1,256]{2,1,0:T(1,128)S(1)}, f32[10,1,256]{2,1,0:T(1,128)S(1)}, u32[]{:S(2)}, u32[]{:S(2)}) collective-permute-start(f32[10,1,256]{2,1,0:T(1,128)S(1)} %get-tuple-element.62), channel_id=1, source_target_pairs={{1,0},{2,1},{3,2},{4,3},{5,4},{6,5},{7,6},{9,8},{10,9},{11,10},{12... | collective-permute-start | bytes 30728 | tf_op jit(solution)/shard_map/ppermute | solution.py:24
  124.8 8.7 %collective-permute-start.11 = (f32[10,1,256]{2,1,0:T(1,128)S(1)}, f32[10,1,256]{2,1,0:T(1,128)S(1)}, u32[]{:S(2)}, u32[]{:S(2)}) collective-permute-start(f32[10,1,256]{2,1,0:T(1,128)S(1)} %get-tuple-element.61), channel_id=1, source_target_pairs={{0,1},{1,2},{2,3},{3,4},{4,5},{5,6},{6,7},{8,9},{9,10},{10,11},{11... | collective-permute-start | bytes 30728 | tf_op jit(solution)/shard_map/ppermute | solution.py:21
  135.3 7.1 %collective-permute-start.16 = (f32[1,16,256]{2,1,0:T(8,128)S(1)}, f32[1,16,256]{2,1,0:T(8,128)S(1)}, u32[]{:S(2)}, u32[]{:S(2)}) collective-permute-start(f32[1,16,256]{2,1,0:T(8,128)S(1)} %get-tuple-element.80), channel_id=1, source_target_pairs={{8,0},{16,8},{24,16},{9,1},{17,9},{25,17},{10,2},{18,10},{26,18},{... | collective-permute-start | bytes 49160 | tf_op jit(solution)/shard_map/ppermute | solution.py:24
  136.6 7.2 %collective-permute-start.17 = (f32[1,16,256]{2,1,0:T(8,128)S(1)}, f32[1,16,256]{2,1,0:T(8,128)S(1)}, u32[]{:S(2)}, u32[]{:S(2)}) collective-permute-start(f32[1,16,256]{2,1,0:T(8,128)S(1)} %get-tuple-element.79), channel_id=1, source_target_pairs={{0,8},{8,16},{16,24},{1,9},{9,17},{17,25},{2,10},{10,18},{18,26},{... | collective-permute-start | bytes 49160 | tf_op jit(solution)/shard_map/ppermute | solution.py:21
  150.0 6.5 %collective-permute-start.20 = (f32[1,16,256]{2,1,0:T(8,128)S(1)}, f32[1,16,256]{2,1,0:T(8,128)S(1)}, u32[]{:S(2)}, u32[]{:S(2)}) collective-permute-start(f32[1,16,256]{2,1,0:T(8,128)S(1)} %get-tuple-element.78), channel_id=1, source_target_pairs={{8,0},{16,8},{24,16},{9,1},{17,9},{25,17},{10,2},{18,10},{26,18},{... | collective-permute-start | bytes 49160 | tf_op jit(solution)/shard_map/ppermute | solution.py:24
  151.3 6.6 %collective-permute-start.21 = (f32[1,16,256]{2,1,0:T(8,128)S(1)}, f32[1,16,256]{2,1,0:T(8,128)S(1)}, u32[]{:S(2)}, u32[]{:S(2)}) collective-permute-start(f32[1,16,256]{2,1,0:T(8,128)S(1)} %get-tuple-element.77), channel_id=1, source_target_pairs={{0,8},{8,16},{16,24},{1,9},{9,17},{17,25},{2,10},{10,18},{18,26},{... | collective-permute-start | bytes 49160 | tf_op jit(solution)/shard_map/ppermute | solution.py:21
  157.9 6.6 %collective-permute-start.22 = (f32[10,1,256]{2,1,0:T(1,128)S(1)}, f32[10,1,256]{2,1,0:T(1,128)S(1)}, u32[]{:S(2)}, u32[]{:S(2)}) collective-permute-start(f32[10,1,256]{2,1,0:T(1,128)S(1)} %get-tuple-element.58), channel_id=1, source_target_pairs={{1,0},{2,1},{3,2},{4,3},{5,4},{6,5},{7,6},{9,8},{10,9},{11,10},{12... | collective-permute-start | bytes 30728 | tf_op jit(solution)/shard_map/ppermute | solution.py:24
  159.2 5.9 %collective-permute-start.23 = (f32[10,1,256]{2,1,0:T(1,128)S(1)}, f32[10,1,256]{2,1,0:T(1,128)S(1)}, u32[]{:S(2)}, u32[]{:S(2)}) collective-permute-start(f32[10,1,256]{2,1,0:T(1,128)S(1)} %get-tuple-element.57), channel_id=1, source_target_pairs={{0,1},{1,2},{2,3},{3,4},{4,5},{5,6},{6,7},{8,9},{9,10},{10,11},{11... | collective-permute-start | bytes 30728 | tf_op jit(solution)/shard_map/ppermute | solution.py:21
  165.5 7.0 %collective-permute-start.24 = (f32[1,16,256]{2,1,0:T(8,128)S(1)}, f32[1,16,256]{2,1,0:T(8,128)S(1)}, u32[]{:S(2)}, u32[]{:S(2)}) collective-permute-start(f32[1,16,256]{2,1,0:T(8,128)S(1)} %get-tuple-element.76), channel_id=1, source_target_pairs={{8,0},{16,8},{24,16},{9,1},{17,9},{25,17},{10,2},{18,10},{26,18},{... | collective-permute-start | bytes 49160 | tf_op jit(solution)/shard_map/ppermute | solution.py:24
  166.8 7.2 %collective-permute-start.25 = (f32[1,16,256]{2,1,0:T(8,128)S(1)}, f32[1,16,256]{2,1,0:T(8,128)S(1)}, u32[]{:S(2)}, u32[]{:S(2)}) collective-permute-start(f32[1,16,256]{2,1,0:T(8,128)S(1)} %get-tuple-element.75), channel_id=1, source_target_pairs={{0,8},{8,16},{16,24},{1,9},{9,17},{17,25},{2,10},{10,18},{18,26},{... | collective-permute-start | bytes 49160 | tf_op jit(solution)/shard_map/ppermute | solution.py:21
  174.0 6.1 %collective-permute-start.26 = (f32[10,1,256]{2,1,0:T(1,128)S(1)}, f32[10,1,256]{2,1,0:T(1,128)S(1)}, u32[]{:S(2)}, u32[]{:S(2)}) collective-permute-start(f32[10,1,256]{2,1,0:T(1,128)S(1)} %get-tuple-element.56), channel_id=1, source_target_pairs={{1,0},{2,1},{3,2},{4,3},{5,4},{6,5},{7,6},{9,8},{10,9},{11,10},{12... | collective-permute-start | bytes 30728 | tf_op jit(solution)/shard_map/ppermute | solution.py:24
  181.3 7.0 %collective-permute-start.28 = (f32[1,16,256]{2,1,0:T(8,128)S(1)}, f32[1,16,256]{2,1,0:T(8,128)S(1)}, u32[]{:S(2)}, u32[]{:S(2)}) collective-permute-start(f32[1,16,256]{2,1,0:T(8,128)S(1)} %get-tuple-element.74), channel_id=1, source_target_pairs={{8,0},{16,8},{24,16},{9,1},{17,9},{25,17},{10,2},{18,10},{26,18},{... | collective-permute-start | bytes 49160 | tf_op jit(solution)/shard_map/ppermute | solution.py:24
  182.6 7.2 %collective-permute-start.29 = (f32[1,16,256]{2,1,0:T(8,128)S(1)}, f32[1,16,256]{2,1,0:T(8,128)S(1)}, u32[]{:S(2)}, u32[]{:S(2)}) collective-permute-start(f32[1,16,256]{2,1,0:T(8,128)S(1)} %get-tuple-element.73), channel_id=1, source_target_pairs={{0,8},{8,16},{16,24},{1,9},{9,17},{17,25},{2,10},{10,18},{18,26},{... | collective-permute-start | bytes 49160 | tf_op jit(solution)/shard_map/ppermute | solution.py:21
  189.8 6.1 %collective-permute-start.30 = (f32[10,1,256]{2,1,0:T(1,128)S(1)}, f32[10,1,256]{2,1,0:T(1,128)S(1)}, u32[]{:S(2)}, u32[]{:S(2)}) collective-permute-start(f32[10,1,256]{2,1,0:T(1,128)S(1)} %get-tuple-element.54), channel_id=1, source_target_pairs={{1,0},{2,1},{3,2},{4,3},{5,4},{6,5},{7,6},{9,8},{10,9},{11,10},{12... | collective-permute-start | bytes 30728 | tf_op jit(solution)/shard_map/ppermute | solution.py:24
  197.2 7.2 %collective-permute-start.32 = (f32[3,1,16,256]{3,2,1,0:T(8,128)S(1)}, f32[3,1,16,256]{3,2,1,0:T(8,128)S(1)}, u32[]{:S(2)}, u32[]{:S(2)}) collective-permute-start(f32[3,1,16,256]{3,2,1,0:T(8,128)S(1)} %get-tuple-element.32), channel_id=1, source_target_pairs={{8,0},{16,8},{24,16},{9,1},{17,9},{25,17},{10,2},{18,10},{26,18},{... | collective-permute-start | bytes 147464 | tf_op jit(solution)/shard_map/ppermute | solution.py:24
  198.5 7.5 %collective-permute-start.33 = (f32[3,1,16,256]{3,2,1,0:T(8,128)S(1)}, f32[3,1,16,256]{3,2,1,0:T(8,128)S(1)}, u32[]{:S(2)}, u32[]{:S(2)}) collective-permute-start(f32[3,1,16,256]{3,2,1,0:T(8,128)S(1)} %get-tuple-element.31), channel_id=1, source_target_pairs={{0,8},{8,16},{16,24},{1,9},{9,17},{17,25},{2,10},{10,18},{18,26},{... | collective-permute-start | bytes 147464 | tf_op jit(solution)/shard_map/ppermute | solution.py:21
  206.1 6.1 %collective-permute-start.34 = (f32[3,10,1,256]{3,2,1,0:T(1,128)S(1)}, f32[3,10,1,256]{3,2,1,0:T(1,128)S(1)}, u32[]{:S(2)}, u32[]{:S(2)}) collective-permute-start(f32[3,10,1,256]{3,2,1,0:T(1,128)S(1)} %get-tuple-element.24), channel_id=1, source_target_pairs={{1,0},{2,1},{3,2},{4,3},{5,4},{6,5},{7,6},{9,8},{10,9},{11,10},{12... | collective-permute-start | bytes 92168 | tf_op jit(solution)/shard_map/ppermute | solution.py:24
  214.2 7.2 %collective-permute-start.36 = (f32[3,1,16,256]{3,2,1,0:T(8,128)S(1)}, f32[3,1,16,256]{3,2,1,0:T(8,128)S(1)}, u32[]{:S(2)}, u32[]{:S(2)}) collective-permute-start(f32[3,1,16,256]{3,2,1,0:T(8,128)S(1)} %get-tuple-element.30), channel_id=1, source_target_pairs={{8,0},{16,8},{24,16},{9,1},{17,9},{25,17},{10,2},{18,10},{26,18},{... | collective-permute-start | bytes 147464 | tf_op jit(solution)/shard_map/ppermute | solution.py:24
  215.5 7.5 %collective-permute-start.37 = (f32[3,1,16,256]{3,2,1,0:T(8,128)S(1)}, f32[3,1,16,256]{3,2,1,0:T(8,128)S(1)}, u32[]{:S(2)}, u32[]{:S(2)}) collective-permute-start(f32[3,1,16,256]{3,2,1,0:T(8,128)S(1)} %get-tuple-element.29), channel_id=1, source_target_pairs={{0,8},{8,16},{16,24},{1,9},{9,17},{17,25},{2,10},{10,18},{18,26},{... | collective-permute-start | bytes 147464 | tf_op jit(solution)/shard_map/ppermute | solution.py:21
  223.1 6.3 %collective-permute-start.38 = (f32[3,10,1,256]{3,2,1,0:T(1,128)S(1)}, f32[3,10,1,256]{3,2,1,0:T(1,128)S(1)}, u32[]{:S(2)}, u32[]{:S(2)}) collective-permute-start(f32[3,10,1,256]{3,2,1,0:T(1,128)S(1)} %get-tuple-element.22), channel_id=1, source_target_pairs={{1,0},{2,1},{3,2},{4,3},{5,4},{6,5},{7,6},{9,8},{10,9},{11,10},{12... | collective-permute-start | bytes 92168 | tf_op jit(solution)/shard_map/ppermute | solution.py:24
  231.1 7.1 %collective-permute-start.40 = (f32[1,16,256]{2,1,0:T(8,128)S(1)}, f32[1,16,256]{2,1,0:T(8,128)S(1)}, u32[]{:S(2)}, u32[]{:S(2)}) collective-permute-start(f32[1,16,256]{2,1,0:T(8,128)S(1)} %get-tuple-element.72), channel_id=1, source_target_pairs={{8,0},{16,8},{24,16},{9,1},{17,9},{25,17},{10,2},{18,10},{26,18},{... | collective-permute-start | bytes 49160 | tf_op jit(solution)/shard_map/ppermute | solution.py:24
  232.4 7.2 %collective-permute-start.41 = (f32[1,16,256]{2,1,0:T(8,128)S(1)}, f32[1,16,256]{2,1,0:T(8,128)S(1)}, u32[]{:S(2)}, u32[]{:S(2)}) collective-permute-start(f32[1,16,256]{2,1,0:T(8,128)S(1)} %get-tuple-element.71), channel_id=1, source_target_pairs={{0,8},{8,16},{16,24},{1,9},{9,17},{17,25},{2,10},{10,18},{18,26},{... | collective-permute-start | bytes 49160 | tf_op jit(solution)/shard_map/ppermute | solution.py:21
  239.6 6.3 %collective-permute-start.42 = (f32[10,1,256]{2,1,0:T(1,128)S(1)}, f32[10,1,256]{2,1,0:T(1,128)S(1)}, u32[]{:S(2)}, u32[]{:S(2)}) collective-permute-start(f32[10,1,256]{2,1,0:T(1,128)S(1)} %get-tuple-element.50), channel_id=1, source_target_pairs={{1,0},{2,1},{3,2},{4,3},{5,4},{6,5},{7,6},{9,8},{10,9},{11,10},{12... | collective-permute-start | bytes 30728 | tf_op jit(solution)/shard_map/ppermute | solution.py:24
  247.1 7.1 %collective-permute-start.44 = (f32[1,16,256]{2,1,0:T(8,128)S(1)}, f32[1,16,256]{2,1,0:T(8,128)S(1)}, u32[]{:S(2)}, u32[]{:S(2)}) collective-permute-start(f32[1,16,256]{2,1,0:T(8,128)S(1)} %get-tuple-element.70), channel_id=1, source_target_pairs={{8,0},{16,8},{24,16},{9,1},{17,9},{25,17},{10,2},{18,10},{26,18},{... | collective-permute-start | bytes 49160 | tf_op jit(solution)/shard_map/ppermute | solution.py:24
  248.4 7.2 %collective-permute-start.45 = (f32[1,16,256]{2,1,0:T(8,128)S(1)}, f32[1,16,256]{2,1,0:T(8,128)S(1)}, u32[]{:S(2)}, u32[]{:S(2)}) collective-permute-start(f32[1,16,256]{2,1,0:T(8,128)S(1)} %get-tuple-element.69), channel_id=1, source_target_pairs={{0,8},{8,16},{16,24},{1,9},{9,17},{17,25},{2,10},{10,18},{18,26},{... | collective-permute-start | bytes 49160 | tf_op jit(solution)/shard_map/ppermute | solution.py:21
  255.6 6.1 %collective-permute-start.46 = (f32[10,1,256]{2,1,0:T(1,128)S(1)}, f32[10,1,256]{2,1,0:T(1,128)S(1)}, u32[]{:S(2)}, u32[]{:S(2)}) collective-permute-start(f32[10,1,256]{2,1,0:T(1,128)S(1)} %get-tuple-element.48), channel_id=1, source_target_pairs={{1,0},{2,1},{3,2},{4,3},{5,4},{6,5},{7,6},{9,8},{10,9},{11,10},{12... | collective-permute-start | bytes 30728 | tf_op jit(solution)/shard_map/ppermute | solution.py:24
  263.0 7.0 %collective-permute-start.48 = (f32[1,16,256]{2,1,0:T(8,128)S(1)}, f32[1,16,256]{2,1,0:T(8,128)S(1)}, u32[]{:S(2)}, u32[]{:S(2)}) collective-permute-start(f32[1,16,256]{2,1,0:T(8,128)S(1)} %get-tuple-element.68), channel_id=1, source_target_pairs={{8,0},{16,8},{24,16},{9,1},{17,9},{25,17},{10,2},{18,10},{26,18},{... | collective-permute-start | bytes 49160 | tf_op jit(solution)/shard_map/ppermute | solution.py:24
  264.3 7.2 %collective-permute-start.49 = (f32[1,16,256]{2,1,0:T(8,128)S(1)}, f32[1,16,256]{2,1,0:T(8,128)S(1)}, u32[]{:S(2)}, u32[]{:S(2)}) collective-permute-start(f32[1,16,256]{2,1,0:T(8,128)S(1)} %get-tuple-element.67), channel_id=1, source_target_pairs={{0,8},{8,16},{16,24},{1,9},{9,17},{17,25},{2,10},{10,18},{18,26},{... | collective-permute-start | bytes 49160 | tf_op jit(solution)/shard_map/ppermute | solution.py:21
  271.5 6.2 %collective-permute-start.50 = (f32[10,1,256]{2,1,0:T(1,128)S(1)}, f32[10,1,256]{2,1,0:T(1,128)S(1)}, u32[]{:S(2)}, u32[]{:S(2)}) collective-permute-start(f32[10,1,256]{2,1,0:T(1,128)S(1)} %get-tuple-element.46), channel_id=1, source_target_pairs={{1,0},{2,1},{3,2},{4,3},{5,4},{6,5},{7,6},{9,8},{10,9},{11,10},{12... | collective-permute-start | bytes 30728 | tf_op jit(solution)/shard_map/ppermute | solution.py:24
  278.9 7.1 %collective-permute-start.52 = (f32[1,16,256]{2,1,0:T(8,128)S(1)}, f32[1,16,256]{2,1,0:T(8,128)S(1)}, u32[]{:S(2)}, u32[]{:S(2)}) collective-permute-start(f32[1,16,256]{2,1,0:T(8,128)S(1)} %get-tuple-element.66), channel_id=1, source_target_pairs={{8,0},{16,8},{24,16},{9,1},{17,9},{25,17},{10,2},{18,10},{26,18},{... | collective-permute-start | bytes 49160 | tf_op jit(solution)/shard_map/ppermute | solution.py:24
  280.2 7.2 %collective-permute-start.53 = (f32[1,16,256]{2,1,0:T(8,128)S(1)}, f32[1,16,256]{2,1,0:T(8,128)S(1)}, u32[]{:S(2)}, u32[]{:S(2)}) collective-permute-start(f32[1,16,256]{2,1,0:T(8,128)S(1)} %get-tuple-element.65), channel_id=1, source_target_pairs={{0,8},{8,16},{16,24},{1,9},{9,17},{17,25},{2,10},{10,18},{18,26},{... | collective-permute-start | bytes 49160 | tf_op jit(solution)/shard_map/ppermute | solution.py:21
  287.3 29.2 %collective-permute-start.54 = (f32[10,1,256]{2,1,0:T(1,128)S(1)}, f32[10,1,256]{2,1,0:T(1,128)S(1)}, u32[]{:S(2)}, u32[]{:S(2)}) collective-permute-start(f32[10,1,256]{2,1,0:T(1,128)S(1)} %get-tuple-element.44), channel_id=1, source_target_pairs={{1,0},{2,1},{3,2},{4,3},{5,4},{6,5},{7,6},{9,8},{10,9},{11,10},{12... | collective-permute-start | bytes 30728 | tf_op jit(solution)/shard_map/ppermute | solution.py:24
  288.6 27.9 %collective-permute-start.55 = (f32[10,1,256]{2,1,0:T(1,128)S(1)}, f32[10,1,256]{2,1,0:T(1,128)S(1)}, u32[]{:S(2)}, u32[]{:S(2)}) collective-permute-start(f32[10,1,256]{2,1,0:T(1,128)S(1)} %get-tuple-element.43), channel_id=1, source_target_pairs={{0,1},{1,2},{2,3},{3,4},{4,5},{5,6},{6,7},{8,9},{9,10},{10,11},{11... | collective-permute-start | bytes 30728 | tf_op jit(solution)/shard_map/ppermute | solution.py:21
  343.7 12.8 %all-to-all-start.2 = ((f32[1,1,8,4,512]{4,3,1,0,2:T(4,128)}), f32[1,1,8,4,512]{4,3,1,0,2:T(4,128)S(1)}, u32[]{:S(2)}, u32[]{:S(2)}) async-start(f32[1,1,8,4,512]{4,3,1,0,2:T(4,128)} %pad_maximum_fusion.105), calls=%async_computation.2 | async-start | bytes 131072 | tf_op jit(solution)/shard_map/all_to_all | solution.py:137
  (35 other events, 362.5 us)
where the time goes:
time: 361 us; the launch traced here: 357 us
  starting transfers between devices  190 us (53%)
  local copies, waits for them, and re-layouts  68.4 us (19%)
  other arithmetic  63.4 us (18%)
  waiting for transfers between devices  33.2 us (9%)
    ppermute x28, starting transfers between devices, extended(): lax.ppermute(lax.slice_in_dim(block, block.shape[dim] - width, None, axis...  136 us
    ppermute x28, starting transfers between devices, extended(): lax.ppermute(lax.slice_in_dim(block, 0, width, axis=dim), axis, backward)  36.2 us
    scatter-add x1, other arithmetic, per_device(): jax.ops.segment_sum(carried, target_field, num_segments=grid_cells)  29.5 us
    ppermute x28, waiting for transfers between devices, extended(): lax.ppermute(lax.slice_in_dim(block, block.shape[dim] - width, None, axis...  23.1 us
    gather x1, local copies, waits for them, and re-layouts, per_device(): flattened_voids[target_field].reshape(slot_shape_factors)  23 us
    scatter-add x1, other arithmetic, per_device(): jax.ops.segment_sum(got_vol.reshape(-1), target_field, num_segments=grid_...  21.9 us
    gather x1, local copies, waits for them, and re-layouts, per_device(): flat_vel[:, target_field].reshape((3,) + slot_shape_factors)  16.5 us
    reshape x1, local copies, waits for them, and re-layouts, per_device(): jax.ops.segment_sum(carried, target_field, num_segments=grid_cells)  9.97 us
  transfers between devices with their start and end apart: 59, of which 26 were waited for; matrix products, arithmetic and copies ran while one was open for 26% of the time, Pallas kernels for 0%

commit v1 on v0

v1 whole, which is shorter than its diff:
```python
import jax
import jax.numpy as jnp
from jax import lax
from jax.experimental import pallas as pl
from jax.experimental.pallas import tpu as pltpu
from jax.sharding import PartitionSpec as P

STEPS = 2
SWEEPS = 4
DRAG = 2.0
DT = 0.25
VISC = 0.2
FLOOR = 0.4

WX = SWEEPS + 1
WY = 8
ROWS = 8

MESH = pl.DeviceIdType.MESH
F32 = jnp.float32
BF16 = jnp.bfloat16


def split(value):
    high = value.astype(BF16).astype(F32)
    return high, value - high


def body(n_gx, n_gy, count_ref, vel_ref, p_ref, cell_ref, gv_ref, vol_ref,
         vel_out, p_out, drag_out,
         v1, v2, pin1, pin2, pa, pb, src1, src2, sp, solid, mf, eps, coef, rate, pull,
         guess, flux, dep, pk, rk, dk, rd, ft, field_send, field_recv, part_send, part_recv):
    bx, by, nz = p_ref.shape
    ex, ey = bx + 2 * WX, by + 2 * WY
    slots = vol_ref.shape[-1]
    columns = bx * by
    ix, iy = lax.axis_index("gx"), lax.axis_index("gy")
    has = {("x", 0): ix > 0, ("x", 1): ix < n_gx - 1, ("y", 0): iy > 0, ("y", 1): iy < n_gy - 1}
    peer = {("x", 0): (ix - 1, iy), ("x", 1): (ix + 1, iy), ("y", 0): (ix, iy - 1), ("y", 1): (ix, iy + 1)}
    own_x, own_y = pl.ds(WX, bx), pl.ds(WY, by)

    barrier = pltpu.get_barrier_semaphore()
    for k in range(1, n_gy):
        pl.semaphore_signal(barrier, inc=1, device_id=(ix, lax.rem(iy + k, n_gy)), device_id_type=MESH)
    for side in (0, 1):
        @pl.when(has["x", side])
        def _():
            pl.semaphore_signal(barrier, inc=1, device_id=peer["x", side], device_id_type=MESH)

    slot = lax.broadcasted_iota(jnp.int32, (1, slots), 1)
    for c in range(n_gy):
        cell = cell_ref[pl.ds(c, 1), :]
        column = lax.div(cell, nz)
        pk[c, 0:1, :] = column.astype(F32)
        pk[c, 1:2, :] = (cell - column * nz).astype(F32)
        pk[c, 2:3, :] = jnp.where(slot < count_ref[c], vol_ref[pl.ds(c, 1), :], 0.0)
        pk[c, 3:6, :] = gv_ref[c]
        pk[c, 6:8, :] = jnp.zeros((2, slots), F32)

    fields = [v1.at[d] for d in range(3)] + [v2.at[d] for d in range(3)] + [mf.at[d] for d in range(3)]
    fields += [pin1, pin2, src1, src2, solid]
    for side in (0, 1):
        @pl.when(jnp.logical_not(has["x", side]))
        def _():
            for field in fields:
                at = 0 if side == 0 else WX + bx
                field[pl.ds(at, WX), own_y, :] = jnp.zeros((WX, by, nz), F32)

        @pl.when(jnp.logical_not(has["y", side]))
        def _():
            for field in fields:
                at = 0 if side == 0 else WY + by
                field[:, pl.ds(at, WY), :] = jnp.zeros((ex, WY, nz), F32)

    pl.semaphore_wait(barrier, n_gy - 1 + jnp.where(ix > 0, 1, 0) + jnp.where(ix < n_gx - 1, 1, 0))

    def particles(k, source, landing, bank):
        return pltpu.make_async_remote_copy(
            src_ref=source, dst_ref=landing, send_sem=part_send.at[bank, k], recv_sem=part_recv.at[bank, k],
            device_id=(ix, lax.rem(iy + k, n_gy)), device_id_type=MESH)

    def outgoing(k):
        return particles(k, pk.at[lax.rem(iy + k, n_gy)], rk.at[iy], 0)

    def incoming(k):
        return particles(k, pk.at[0], rk.at[lax.rem(iy + n_gy - k, n_gy)], 0)

    for k in range(1, n_gy):
        outgoing(k).start()
    rk[iy] = pk[iy]

    class Halo:
        def __init__(self, slot, ref, width, own=None, corners=True):
            self.slot, self.ref, self.width, self.own, self.corners = slot, ref, width, own, corners

        def copy(self, index, source, landing, to):
            return pltpu.make_async_remote_copy(
                src_ref=source, dst_ref=landing, send_sem=field_send.at[self.slot, index],
                recv_sem=field_recv.at[self.slot, index], device_id=to, device_id_type=MESH)

        def x_copy(self, side):
            w = self.width
            at = 0 if side == 0 else bx - w
            if self.own is None:
                source = self.ref.at[pl.ds(WX + at, w), own_y]
            else:
                source = self.own.at[pl.ds(at, w)]
            landing = self.ref.at[pl.ds(WX + bx if side == 0 else WX - w, w), own_y]
            return self.copy(side, source, landing, peer["x", side])

        def y_copy(self, side):
            at = 0 if side == 0 else by - WY
            if self.own is None:
                source = self.ref.at[own_x, pl.ds(WY + at, WY)]
            else:
                source = self.own.at[:, pl.ds(at, WY)]
            landing = self.ref.at[own_x, pl.ds(WY + by if side == 0 else 0, WY)]
            return self.copy(2 + side, source, landing, peer["y", side])

        def c_copy(self, side, end):
            w = self.width
            rows = pl.ds(WX - w if end == 0 else WX + bx, w)
            source = self.ref.at[rows, pl.ds(WY if side == 0 else by, WY)]
            landing = self.ref.at[rows, pl.ds(WY + by if side == 0 else 0, WY)]
            return self.copy(4 + 2 * side + end, source, landing, peer["y", side])

        def each(self, axis, act, flip=False):
            for side in (0, 1):
                @pl.when(has[axis, 1 - side if flip else side])
                def _():
                    if axis == "x":
                        act(self.x_copy(side))
                    else:
                        act(self.y_copy(side))

        def each_corner(self, act, flip=False):
            for side in (0, 1):
                @pl.when(has["y", 1 - side if flip else side])
                def _():
                    for end in (0, 1):
                        act(self.c_copy(side, end))

    sent = []

    def start(halos):
        for h in halos:
            h.each("x", lambda c: c.start())
        for h in halos:
            h.each("y", lambda c: c.start())
        sent.extend(halos)

    def relay(halos):
        for h in halos:
            h.each("x", lambda c: c.wait_recv(), flip=True)
            if h.corners:
                h.each_corner(lambda c: c.start())

    def arrive(halos):
        for h in halos:
            h.each("y", lambda c: c.wait_recv(), flip=True)
            if h.corners:
                h.each_corner(lambda c: c.wait_recv(), flip=True)

    h_vel = [[Halo(0, v1.at[0], 2, vel_ref.at[0]), Halo(1, v1.at[1], 1, vel_ref.at[1]), Halo(2, v1.at[2], 1, vel_ref.at[2], False)],
             [Halo(3, v2.at[0], 2), Halo(4, v2.at[1], 1), Halo(5, v2.at[2], 1, None, False)]]
    h_p = [[Halo(6, pin1, WX, p_ref)], [Halo(7, pin2, WX)]]
    h_src = [[Halo(8, src1, SWEEPS)], [Halo(9, src2, SWEEPS)]]
    h_solid = [Halo(10, solid, WX)]
    h_mf = [Halo(11, mf.at[0], 1, None, False), Halo(12, mf.at[1], 1, None, False)]

    start(h_vel[0] + h_p[0])
    for d in range(3):
        v1[d, own_x, own_y, :] = vel_ref[d]
    pin1[own_x, own_y, :] = p_ref[...]

    column_of = lax.broadcasted_iota(jnp.int32, (columns, slots), 0).astype(F32)
    depth_of = lax.broadcasted_iota(jnp.int32, (nz, slots), 0).astype(F32)
    dep[...] = jnp.zeros_like(dep)
    for k in range(1, n_gy):
        incoming(k).wait_recv()

    def deposit(b, carry):
        hot_c = rk[b, 0:1, :] == column_of
        hot_z = jnp.where(rk[b, 1:2, :] == depth_of, 1.0, 0.0).astype(BF16)
        volume = rk[b, 2:3, :]
        values = [volume] + [volume * rk[b, 3 + d:4 + d, :] for d in range(3)]
        parts = [split(value) for value in values]
        both = None
        for side in (0, 1):
            left = jnp.concatenate([jnp.where(hot_c, part[side], 0.0).astype(BF16) for part in parts], axis=0)
            term = lax.dot_general(left, hot_z, (((1,), (1,)), ((), ())), preferred_element_type=F32)
            both = term if both is None else both + term
        dep[...] += both
        return carry

    lax.fori_loop(0, n_gy, deposit, 0)
    solid[own_x, own_y, :] = dep[pl.ds(0, columns), :].reshape(bx, by, nz)
    for d in range(3):
        mf[d, own_x, own_y, :] = dep[pl.ds((1 + d) * columns, columns), :].reshape(bx, by, nz)
    start(h_solid + h_mf)
    relay(h_vel[0])
    relay(h_p[0])
    relay(h_solid + h_mf)
    arrive(h_solid + h_mf)
    arrive(h_vel[0])

    row = lax.broadcasted_iota(jnp.int32, (ey, nz), 0)
    depth = lax.broadcasted_iota(jnp.int32, (ey, nz), 1)
    row_in = jnp.where((row >= WY) | (iy > 0), 1.0, 0.0) * jnp.where((row < WY + by) | (iy < n_gy - 1), 1.0, 0.0)

    def voidage(x, carry):
        x_in = ((x >= WX) | (ix > 0)) & ((x < WX + bx) | (ix < n_gx - 1))
        eps[x] = jnp.maximum(1.0 - solid[x], FLOOR) * (row_in * jnp.where(x_in, 1.0, 0.0))
        return carry

    lax.fori_loop(0, ex, voidage, 0)

    def up_y(v):
        return pltpu.roll(v, ey - 1, 0)

    def down_y(v):
        return pltpu.roll(v, 1, 0)

    def up_z(v):
        return pltpu.roll(v, nz - 1, 1)

    def down_z(v):
        return pltpu.roll(v, 1, 1)

    last_z, first_z = depth == nz - 1, depth == 0

    def weights(x, carry):
        e = eps[x]
        near = [eps[x + 1], eps[x - 1], up_y(e), down_y(e),
                jnp.where(last_z, 0.0, up_z(e)), jnp.where(first_z, 0.0, down_z(e))]
        total = 0.5 * (6.0 * e + (((near[0] + near[1]) + (near[2] + near[3])) + (near[4] + near[5])))
        inside = e > 0.0
        inverse = jnp.where(inside, 0.5 / jnp.where(inside, total, 1.0), 0.0)
        for n in range(6):
            w = (e + near[n]) * inverse
            if n == 4:
                w = jnp.where(last_z, 0.0, w)
            if n == 5:
                w = jnp.where(first_z, 0.0, w)
            coef[n, x] = w
        coef[6, x] = 2.0 * inverse
        recip = 1.0 / jnp.where(inside, e, 1.0)
        rate[x] = (DT * VISC) * total * recip
        pull[x] = (DT * DRAG) * recip
        return carry

    lax.fori_loop(1, ex - 1, weights, 0)

    def stencil(field, x):
        v = field[x]
        return v, (((coef[0, x] * field[x + 1] + coef[1, x] * field[x - 1])
                    + (coef[2, x] * up_y(v) + coef[3, x] * down_y(v)))
                   + (coef[4, x] * up_z(v) + coef[5, x] * down_z(v)))

    for step in range(STEPS):
        v = (v1, v2)[step]
        pin = (pin1, pin2)[step]
        src = (src1, src2)[step]

        def predict(x, carry):
            s, r, g, e = solid[x], rate[x], pull[x], eps[x]
            for d in range(3):
                old, mean = stencil(v.at[d], x)
                new = old + r * (mean - old) + g * (mf[d, x] - s * old)
                guess[d, x] = new
                flux[d, x] = e * new
            return carry

        lax.fori_loop(WX - 1, WX + bx + 1, predict, 0)

        def balance(x, carry):
            f1, f2 = flux[1, x], flux[2, x]
            out = ((flux[0, x + 1] - flux[0, x - 1]) + (up_y(f1) - down_y(f1))
                   + (jnp.where(last_z, 0.0, up_z(f2)) - jnp.where(first_z, 0.0, down_z(f2))))
            src[x, own_y, :] = (0.5 / DT) * out[WY:WY + by]
            return carry

        lax.fori_loop(WX, WX + bx, balance, 0)
        start(h_src[step])
        if step > 0:
            relay(h_p[step])
        relay(h_src[step])
        arrive(h_p[step])
        arrive(h_src[step])

        def scale(x, carry):
            sp[x] = src[x] * coef[6, x]
            return carry

        lax.fori_loop(1, ex - 1, scale, 0)

        held = pin
        for sweep in range(SWEEPS):
            into = (pa, pb)[sweep % 2]

            def relax(x, carry):
                _, mean = stencil(held, x)
                into[x] = mean - sp[x]
                return carry

            lax.fori_loop(1 + sweep, ex - 1 - sweep, relax, 0)
            held = into

        final = step == STEPS - 1

        def correct(x, carry):
            p = held[x]
            slopes = [held[x + 1] - held[x - 1], up_y(p) - down_y(p),
                      jnp.where(last_z, 0.0, up_z(p)) - jnp.where(first_z, 0.0, down_z(p))]
            for d in range(3):
                new = (guess[d, x] - (0.5 * DT) * slopes[d])[WY:WY + by]
                if final:
                    vel_out[d, x - WX] = new
                else:
                    v2[d, x, own_y, :] = new
            if final:
                p_out[x - WX] = p[WY:WY + by]
            else:
                pin2[x, own_y, :] = p[WY:WY + by]
            return carry

        lax.fori_loop(WX, WX + bx, correct, 0)
        if not final:
            start(h_vel[step + 1])
            start(h_p[step + 1])
            relay(h_vel[step + 1])
            arrive(h_vel[step + 1])

    for f in range(4):
        grid = (vel_out[f] if f < 3 else eps[own_x, own_y, :]).reshape(columns, nz)
        high, low = split(grid.T)
        ft[pl.ds(f * nz, nz), :] = jnp.concatenate([high.astype(BF16), low.astype(BF16)], axis=1)

    def gather(b, carry):
        hot = jnp.where(rk[b, 0:1, :] == column_of, 1.0, 0.0).astype(BF16)
        hot_z = rk[b, 1:2, :] == depth_of
        wide = jnp.dot(ft[...], jnp.concatenate([hot, hot], axis=0), preferred_element_type=F32)
        at = [jnp.sum(jnp.where(hot_z, wide[f * nz:(f + 1) * nz], 0.0), axis=0, keepdims=True) for f in range(4)]
        scaled = rk[b, 2:3, :] * DRAG
        for d in range(3):
            dk[b, d:d + 1, :] = scaled * (at[d] - rk[b, 3 + d:4 + d, :]) / at[3]
        return carry

    lax.fori_loop(0, n_gy, gather, 0)

    def giving(k):
        return particles(k, dk.at[lax.rem(iy + k, n_gy)], rd.at[iy], 1)

    def getting(k):
        return particles(k, dk.at[0], rd.at[lax.rem(iy + n_gy - k, n_gy)], 1)

    for k in range(1, n_gy):
        giving(k).start()
    rd[iy] = dk[iy]
    for h in sent:
        h.each("x", lambda c: c.wait_send())
        h.each("y", lambda c: c.wait_send())
        if h.corners:
            h.each_corner(lambda c: c.wait_send())
    for k in range(1, n_gy):
        outgoing(k).wait_send()
        getting(k).wait_recv()
        giving(k).wait_send()
    for c in range(n_gy):
        drag_out[c] = rd[c, 0:3, :]


def solution(mesh):
    n_gx, n_gy = mesh.shape["gx"], mesh.shape["gy"]

    def per_device(velocity, pressure, part_cell, part_count, grain_velocities, part_vol):
        bx, by, nz = pressure.shape
        slots = part_vol.shape[-1]
        ext = (bx + 2 * WX, by + 2 * WY, nz)
        vmem = pl.BlockSpec(memory_space=pltpu.VMEM)

        def field(*lead):
            return pltpu.VMEM(lead + ext, F32)

        def kernel(*refs):
            body(n_gx, n_gy, *refs)

        v, p, drag = pl.pallas_call(
            kernel,
            name="interval",
            out_shape=(
                jax.ShapeDtypeStruct(velocity.shape, F32),
                jax.ShapeDtypeStruct(pressure.shape, F32),
                jax.ShapeDtypeStruct((n_gy, 3, slots), F32),
            ),
            in_specs=[pl.BlockSpec(memory_space=pltpu.SMEM)] + [vmem] * 5,
            out_specs=(vmem,) * 3,
            scratch_shapes=[
                field(3), field(3), field(), field(), field(), field(), field(), field(), field(),
                field(), field(3), field(), field(7), field(), field(), field(3), field(3),
                pltpu.VMEM((4 * bx * by, nz), F32),
                pltpu.VMEM((n_gy, ROWS, slots), F32),
                pltpu.VMEM((n_gy, ROWS, slots), F32),
                pltpu.VMEM((n_gy, 3, slots), F32),
                pltpu.VMEM((n_gy, 3, slots), F32),
                pltpu.VMEM((4 * nz, 2 * bx * by), BF16),
                pltpu.SemaphoreType.DMA((13, 8)),
                pltpu.SemaphoreType.DMA((13, 8)),
                pltpu.SemaphoreType.DMA((2, n_gy)),
                pltpu.SemaphoreType.DMA((2, n_gy)),
            ],
            compiler_params=pltpu.CompilerParams(
                collective_id=0, has_side_effects=True, vmem_limit_bytes=56 * 1024 * 1024
            ),
        )(
            part_count.reshape(n_gy),
            velocity,
            pressure,
            part_cell.reshape(n_gy, slots),
            grain_velocities.reshape(n_gy, 3, slots),
            part_vol.reshape(n_gy, slots),
        )
        return v, p, drag.reshape(grain_velocities.shape)

    placed = (
        P(None, "gx", "gy", None),
        P("gx", "gy", None),
        P("gx", "gy", None, None),
        P("gx", "gy", None),
        P("gx", "gy", None, None, None),
        P("gx", "gy", None, None),
    )
    return jax.shard_map(
        per_device,
        mesh=mesh,
        in_specs=placed,
        out_specs=(P(None, "gx", "gy", None), P("gx", "gy", None), P("gx", "gy", None, None, None)),
        check_vma=False,
    )
```

time: 361 us -> 76.5 us (0.21)
  starting transfers between devices: 190 us -> 0 us
  Pallas kernels: 0 us -> 70.2 us
  other arithmetic: 63.4 us -> 0 us
  local copies, waits for them, and re-layouts: 68.4 us -> 5.4 us
  waiting for transfers between devices: 33.2 us -> 0 us
    ppermute x56 -> x0, starting transfers between devices: 172 us -> none  [the longest x28 136 us: extended(): lax.ppermute(lax.slice_in_dim(block, block.shape[dim] - width, None, axis...]
    pallas_call x0 -> x1, Pallas kernels: none -> 70.2 us  [per_device(): pl.pallas_call(kernel, name='interval', out_shape=(jax.ShapeDtypeStruct(v...]
    scatter-add x2 -> x0, other arithmetic: 51.5 us -> none  [the longest x1 29.5 us: per_device(): jax.ops.segment_sum(carried, target_field, num_segments=grid_cells)]
    gather x2 -> x0, local copies, waits for them, and re-layouts: 39.6 us -> none  [the longest x1 23 us: per_device(): flattened_voids[target_field].reshape(slot_shape_factors)]
    ppermute x56 -> x0, waiting for transfers between devices: 26.1 us -> none  [the longest x28 23.1 us: extended(): lax.ppermute(lax.slice_in_dim(block, block.shape[dim] - width, None, axis...]
    all_to_all x3 -> x0, starting transfers between devices: 18.3 us -> none  [the longest x1 6.86 us: per_device(): lax.all_to_all(coupled_state, 'gy', split_axis=2, concat_axis=2, tiled=True)]
    reshape x4 -> x0, local copies, waits for them, and re-layouts: 12.6 us -> none  [the longest x1 9.97 us: per_device(): jax.ops.segment_sum(carried, target_field, num_segments=grid_cells)]
    sub x1 -> x0, local copies, waits for them, and re-layouts: 8.74 us -> none  [per_device(): velocity = guess - time_step * gradient(padding_thickness(slope_cycle))]
  transfers between devices with their start and end apart: 59 -> 0, of which waited for: 26 -> 0; matrix products, arithmetic and copies ran while one was open for 26% -> 0% of each run, Pallas kernels for 0% -> 0%
where the time goes in v1:
time: 76.5 us; the launch traced here: 76.3 us
  Pallas kernels  70.2 us (92%)
  local copies, waits for them, and re-layouts  5.4 us (7%)
    pallas_call x1, Pallas kernels, per_device(): pl.pallas_call(kernel, name='interval', out_shape=(jax.ShapeDtypeStruct(v...  70.2 us
    unnamed x6, local copies, waits for them, and re-layouts  5.4 us

profile of v1, /device:TPU:0, one launch (start us, length us, event | category | flops | bytes accessed | tf_op | source)
XLA Modules:
  0.0 76.3 jit_solution(16068449200788024150)
XLA Ops:
  0.6 1.5 %copy.12 = f32[1,1,8,3,512]{4,3,2,1,0:T(4,128)} copy(f32[1,1,8,3,512]{4,2,3,1,0:T(8,128)} %param.10) | data formatting | bytes 98304 | tf_op args[4]
  2.1 70.2 %interval.1 = (f32[3,8,16,256]{3,2,1,0:T(8,128)}, f32[8,16,256]{2,1,0:T(8,128)}, f32[8,3,512]{2,1,0:T(4,128)}) custom-call(s32[8]{0:T(128)} %bitcast.11, f32[3,8,16,256]{3,2,1,0:T(8,128)} %refs_1_.1, f32[8,16,256]{2,1,0:T(8,128)} %refs_2_.1, s32[8,512]{1,0:T(8,128)} %bitcast.9, f32[8,3,512]{2,1,0:T(4,128)} %bitcast.7, f32[8,512]{1,0:T(8,128)} %bitcast.10), custom_call_target="tpu_custom_call" | custom-call | tf_op jit(solution)/shard_map/interval/pallas_call | solution.py:388
  72.3 1.5 %copy.10 = f32[1,1,8,3,512]{4,2,3,1,0:T(8,128)} copy(f32[1,1,8,3,512]{4,3,2,1,0:T(4,128)} %bitcast.8) | data formatting | bytes 98304
  73.8 0.0 copy-start
  73.8 1.8 %copy.15 = f32[3,8,16,256]{3,2,1,0:T(8,128)} copy(f32[3,8,16,256]{3,2,1,0:T(8,128)} %get-tuple-element.15) | data formatting | bytes 786432
  75.6 0.0 copy-done
  75.6 0.7 copy.16
Async XLA Ops:
  73.8 1.8 %copy-start = (f32[8,16,256]{2,1,0:T(8,128)S(1)}, f32[8,16,256]{2,1,0:T(8,128)}, u32[]{:S(2)}) copy-start(f32[8,16,256]{2,1,0:T(8,128)} %get-tuple-element.16) | copy-start | bytes 393220

commit v2 on v1

--- a/solution.py
+++ b/solution.py
@@ -17,6 +17,7 @@
 ROWS = 8
 
 MESH = pl.DeviceIdType.MESH
+CORNERS = ((0, 0), (0, 1), (1, 0), (1, 1))
 F32 = jnp.float32
 BF16 = jnp.bfloat16
 
@@ -29,7 +30,7 @@
 def body(n_gx, n_gy, count_ref, vel_ref, p_ref, cell_ref, gv_ref, vol_ref,
          vel_out, p_out, drag_out,
          v1, v2, pin1, pin2, pa, pb, src1, src2, sp, solid, mf, eps, coef, rate, pull,
-         guess, flux, dep, pk, rk, dk, rd, ft, field_send, field_recv, part_send, part_recv):
+         guess, flux, dep, pk, rk, dk, rd, ft, corner_out, corner_in, field_send, field_recv, part_send, part_recv):
     bx, by, nz = p_ref.shape
     ex, ey = bx + 2 * WX, by + 2 * WY
     slots = vol_ref.shape[-1]
@@ -39,6 +40,9 @@
     peer = {("x", 0): (ix - 1, iy), ("x", 1): (ix + 1, iy), ("y", 0): (ix, iy - 1), ("y", 1): (ix, iy + 1)}
     own_x, own_y = pl.ds(WX, bx), pl.ds(WY, by)
 
+    def beyond(corner):
+        return ix + (2 * corner[0] - 1), iy + (2 * corner[1] - 1)
+
     barrier = pltpu.get_barrier_semaphore()
     for k in range(1, n_gy):
         pl.semaphore_signal(barrier, inc=1, device_id=(ix, lax.rem(iy + k, n_gy)), device_id_type=MESH)
@@ -46,6 +50,10 @@
         @pl.when(has["x", side])
         def _():
             pl.semaphore_signal(barrier, inc=1, device_id=peer["x", side], device_id_type=MESH)
+    for corner in CORNERS:
+        @pl.when(has["x", corner[0]] & has["y", corner[1]])
+        def _():
+            pl.semaphore_signal(barrier, inc=1, device_id=beyond(corner), device_id_type=MESH)
 
     slot = lax.broadcasted_iota(jnp.int32, (1, slots), 1)
     for c in range(n_gy):
@@ -54,7 +62,8 @@
         pk[c, 0:1, :] = column.astype(F32)
         pk[c, 1:2, :] = (cell - column * nz).astype(F32)
         pk[c, 2:3, :] = jnp.where(slot < count_ref[c], vol_ref[pl.ds(c, 1), :], 0.0)
-        pk[c, 3:6, :] = gv_ref[c]
+        for d in range(3):
+            pk[c, 3 + d:4 + d, :] = gv_ref[d, pl.ds(c, 1), :]
         pk[c, 6:8, :] = jnp.zeros((2, slots), F32)
 
     fields = [v1.at[d] for d in range(3)] + [v2.at[d] for d in range(3)] + [mf.at[d] for d in range(3)]
@@ -64,7 +73,7 @@
         def _():
             for field in fields:
                 at = 0 if side == 0 else WX + bx
-                field[pl.ds(at, WX), own_y, :] = jnp.zeros((WX, by, nz), F32)
+                field[pl.ds(at, WX)] = jnp.zeros((WX, ey, nz), F32)
 
         @pl.when(jnp.logical_not(has["y", side]))
         def _():
@@ -72,7 +81,9 @@
                 at = 0 if side == 0 else WY + by
                 field[:, pl.ds(at, WY), :] = jnp.zeros((ex, WY, nz), F32)
 
-    pl.semaphore_wait(barrier, n_gy - 1 + jnp.where(ix > 0, 1, 0) + jnp.where(ix < n_gx - 1, 1, 0))
+    x_peers = jnp.where(ix > 0, 1, 0) + jnp.where(ix < n_gx - 1, 1, 0)
+    y_peers = jnp.where(iy > 0, 1, 0) + jnp.where(iy < n_gy - 1, 1, 0)
+    pl.semaphore_wait(barrier, n_gy - 1 + x_peers * (1 + y_peers))
 
     def particles(k, source, landing, bank):
         return pltpu.make_async_remote_copy(
@@ -90,8 +101,9 @@
     rk[iy] = pk[iy]
 
     class Halo:
-        def __init__(self, slot, ref, width, own=None, corners=True):
-            self.slot, self.ref, self.width, self.own, self.corners = slot, ref, width, own, corners
+        def __init__(self, slot, ref, width, reach=0, own=None, axes="xy", skip=0):
+            self.slot, self.ref, self.width, self.own, self.axes, self.skip = slot, ref, width, own, axes, skip
+            self.rows = [(i, j) for i in range(reach) for j in range(reach) if i + j + 2 <= reach]
 
         def copy(self, index, source, landing, to):
             return pltpu.make_async_remote_copy(
@@ -99,13 +111,13 @@
                 recv_sem=field_recv.at[self.slot, index], device_id=to, device_id_type=MESH)
 
         def x_copy(self, side):
-            w = self.width
-            at = 0 if side == 0 else bx - w
+            w, skip = self.width, self.skip
+            at = skip if side == 0 else bx - w - skip
             if self.own is None:
                 source = self.ref.at[pl.ds(WX + at, w), own_y]
             else:
                 source = self.own.at[pl.ds(at, w)]
-            landing = self.ref.at[pl.ds(WX + bx if side == 0 else WX - w, w), own_y]
+            landing = self.ref.at[pl.ds(WX + bx + skip if side == 0 else WX - w - skip, w), own_y]
             return self.copy(side, source, landing, peer["x", side])
 
         def y_copy(self, side):
@@ -117,68 +129,73 @@
             landing = self.ref.at[own_x, pl.ds(WY + by if side == 0 else 0, WY)]
             return self.copy(2 + side, source, landing, peer["y", side])
 
-        def c_copy(self, side, end):
-            w = self.width
-            rows = pl.ds(WX - w if end == 0 else WX + bx, w)
-            source = self.ref.at[rows, pl.ds(WY if side == 0 else by, WY)]
-            landing = self.ref.at[rows, pl.ds(WY + by if side == 0 else 0, WY)]
-            return self.copy(4 + 2 * side + end, source, landing, peer["y", side])
+        def c_copy(self, corner):
+            n = 2 * corner[0] + corner[1]
+            size = -(-len(self.rows) // 8) * 8
+            return self.copy(4 + n, corner_out.at[self.slot, n, pl.ds(0, size)],
+                             corner_in.at[self.slot, n, pl.ds(0, size)], beyond(corner))
+
+        def pack(self):
+            for corner in CORNERS if self.rows else ():
+                for n, (i, j) in enumerate(self.rows):
+                    x = WX + (i if corner[0] == 0 else bx - 1 - i)
+                    y = WY + (j if corner[1] == 0 else by - 1 - j)
+                    corner_out[self.slot, 2 * corner[0] + corner[1], n:n + 1, :] = self.ref[x, y:y + 1, :]
 
         def each(self, axis, act, flip=False):
-            for side in (0, 1):
-                @pl.when(has[axis, 1 - side if flip else side])
-                def _():
-                    if axis == "x":
-                        act(self.x_copy(side))
-                    else:
-                        act(self.y_copy(side))
-
-        def each_corner(self, act, flip=False):
-            for side in (0, 1):
-                @pl.when(has["y", 1 - side if flip else side])
-                def _():
-                    for end in (0, 1):
-                        act(self.c_copy(side, end))
+            if axis == "c":
+                for corner in CORNERS if self.rows else ():
+                    near = (1 - corner[0], 1 - corner[1]) if flip else corner
+
+                    @pl.when(has["x", near[0]] & has["y", near[1]])
+                    def _():
+                        act(self.c_copy(corner), corner)
+            elif axis in self.axes:
+                for side in (0, 1):
+                    @pl.when(has[axis, 1 - side if flip else side])
+                    def _():
+                        act((self.x_copy if axis == "x" else self.y_copy)(side), None)
+
+        def unpack(self, copy, corner):
+            copy.wait_recv()
+            for n, (i, j) in enumerate(self.rows):
+                x = WX + bx + i if corner[0] == 0 else WX - 1 - i
+                y = WY + by + j if corner[1] == 0 else WY - 1 - j
+                self.ref[x, y:y + 1, :] = corner_in[self.slot, 2 * corner[0] + corner[1], n:n + 1, :]
 
     sent = []
 
     def start(halos):
         for h in halos:
-            h.each("x", lambda c: c.start())
-        for h in halos:
-            h.each("y", lambda c: c.start())
+            h.pack()
+        for axis in "xcy":
+            for h in halos:
+                h.each(axis, lambda c, _: c.start())
         sent.extend(halos)
-
-    def relay(halos):
-        for h in halos:
-            h.each("x", lambda c: c.wait_recv(), flip=True)
-            if h.corners:
-                h.each_corner(lambda c: c.start())
 
     def arrive(halos):
         for h in halos:
-            h.each("y", lambda c: c.wait_recv(), flip=True)
-            if h.corners:
-                h.each_corner(lambda c: c.wait_recv(), flip=True)
-
-    h_vel = [[Halo(0, v1.at[0], 2, vel_ref.at[0]), Halo(1, v1.at[1], 1, vel_ref.at[1]), Halo(2, v1.at[2], 1, vel_ref.at[2], False)],
-             [Halo(3, v2.at[0], 2), Halo(4, v2.at[1], 1), Halo(5, v2.at[2], 1, None, False)]]
-    h_p = [[Halo(6, pin1, WX, p_ref)], [Halo(7, pin2, WX)]]
-    h_src = [[Halo(8, src1, SWEEPS)], [Halo(9, src2, SWEEPS)]]
-    h_solid = [Halo(10, solid, WX)]
-    h_mf = [Halo(11, mf.at[0], 1, None, False), Halo(12, mf.at[1], 1, None, False)]
-
-    start(h_vel[0] + h_p[0])
+            h.each("y", lambda c, _: c.wait_recv(), flip=True)
+            h.each("x", lambda c, _: c.wait_recv(), flip=True)
+        for h in halos:
+            h.each("c", h.unpack, flip=True)
+
+    h_vel = [[Halo(0, v1.at[0], 2, 2, vel_ref.at[0]), Halo(1, v1.at[1], 1, 2, vel_ref.at[1]), Halo(2, v1.at[2], 1, 0, vel_ref.at[2])],
+             [Halo(3, v2.at[0], 2, 2), Halo(4, v2.at[1], 1, 2), Halo(5, v2.at[2], 1)]]
+    h_p = [[Halo(6, pin1, WX, WX, p_ref)], [Halo(7, pin2, WX, WX)]]
+    h_src = [[Halo(8, src1, SWEEPS, SWEEPS)], [Halo(9, src2, SWEEPS, SWEEPS)]]
+    h_solid = [Halo(10, solid, 2, WX)]
+    h_rest = [Halo(13, solid, WX - 2, axes="x", skip=2)]
+    h_mf = [Halo(11, mf.at[0], 1, axes="x"), Halo(12, mf.at[1], 1, axes="y")]
+
     for d in range(3):
         v1[d, own_x, own_y, :] = vel_ref[d]
     pin1[own_x, own_y, :] = p_ref[...]
+    start(h_vel[0] + h_p[0])
 
     column_of = lax.broadcasted_iota(jnp.int32, (columns, slots), 0).astype(F32)
     depth_of = lax.broadcasted_iota(jnp.int32, (nz, slots), 0).astype(F32)
     dep[...] = jnp.zeros_like(dep)
-    for k in range(1, n_gy):
-        incoming(k).wait_recv()
-
     def deposit(b, carry):
         hot_c = rk[b, 0:1, :] == column_of
         hot_z = jnp.where(rk[b, 1:2, :] == depth_of, 1.0, 0.0).astype(BF16)
@@ -193,14 +210,18 @@
         dep[...] += both
         return carry
 
-    lax.fori_loop(0, n_gy, deposit, 0)
+    deposit(iy, 0)
+
+    def deposit_from(k, carry):
+        incoming(k).wait_recv()
+        return deposit(lax.rem(iy + n_gy - k, n_gy), carry)
+
+    lax.fori_loop(1, n_gy, deposit_from, 0)
     solid[own_x, own_y, :] = dep[pl.ds(0, columns), :].reshape(bx, by, nz)
     for d in range(3):
         mf[d, own_x, own_y, :] = dep[pl.ds((1 + d) * columns, columns), :].reshape(bx, by, nz)
     start(h_solid + h_mf)
-    relay(h_vel[0])
-    relay(h_p[0])
-    relay(h_solid + h_mf)
+    start(h_rest)
     arrive(h_solid + h_mf)
     arrive(h_vel[0])
 
@@ -213,7 +234,7 @@
         eps[x] = jnp.maximum(1.0 - solid[x], FLOOR) * (row_in * jnp.where(x_in, 1.0, 0.0))
         return carry
 
-    lax.fori_loop(0, ex, voidage, 0)
+    lax.fori_loop(WX - 2, WX + bx + 2, voidage, 0, unroll=4)
 
     def up_y(v):
         return pltpu.roll(v, ey - 1, 0)
@@ -249,7 +270,7 @@
         pull[x] = (DT * DRAG) * recip
         return carry
 
-    lax.fori_loop(1, ex - 1, weights, 0)
+    lax.fori_loop(WX - 1, WX + bx + 1, weights, 0, unroll=5)
 
     def stencil(field, x):
         v = field[x]
@@ -271,7 +292,7 @@
                 flux[d, x] = e * new
             return carry
 
-        lax.fori_loop(WX - 1, WX + bx + 1, predict, 0)
+        lax.fori_loop(WX - 1, WX + bx + 1, predict, 0, unroll=5)
 
         def balance(x, carry):
             f1, f2 = flux[1, x], flux[2, x]
@@ -280,11 +301,14 @@
             src[x, own_y, :] = (0.5 / DT) * out[WY:WY + by]
             return carry
 
-        lax.fori_loop(WX, WX + bx, balance, 0)
+        lax.fori_loop(WX, WX + bx, balance, 0, unroll=8)
         start(h_src[step])
-        if step > 0:
-            relay(h_p[step])
-        relay(h_src[step])
+        if step == 0:
+            arrive(h_rest)
+            for low in (0, WX + bx + 2):
+                lax.fori_loop(low, low + WX - 2, voidage, 0, unroll=3)
+            for low in (1, WX + bx + 1):
+                lax.fori_loop(low, low + WX - 2, weights, 0, unroll=3)
         arrive(h_p[step])
         arrive(h_src[step])
 
@@ -292,7 +316,7 @@
             sp[x] = src[x] * coef[6, x]
             return carry
 
-        lax.fori_loop(1, ex - 1, scale, 0)
+        lax.fori_loop(1, ex - 1, scale, 0, unroll=8)
 
         held = pin
         for sweep in range(SWEEPS):
@@ -303,7 +327,7 @@
                 into[x] = mean - sp[x]
                 return carry
 
-            lax.fori_loop(1 + sweep, ex - 1 - sweep, relax, 0)
+            lax.fori_loop(1 + sweep, ex - 1 - sweep, relax, 0, unroll=4)
             held = into
 
         final = step == STEPS - 1
@@ -324,11 +348,10 @@
                 pin2[x, own_y, :] = p[WY:WY + by]
             return carry
 
-        lax.fori_loop(WX, WX + bx, correct, 0)
+        lax.fori_loop(WX, WX + bx, correct, 0, unroll=4)
         if not final:
             start(h_vel[step + 1])
             start(h_p[step + 1])
-            relay(h_vel[step + 1])
             arrive(h_vel[step + 1])
 
     for f in range(4):
@@ -346,28 +369,30 @@
             dk[b, d:d + 1, :] = scaled * (at[d] - rk[b, 3 + d:4 + d, :]) / at[3]
         return carry
 
-    lax.fori_loop(0, n_gy, gather, 0)
-
     def giving(k):
         return particles(k, dk.at[lax.rem(iy + k, n_gy)], rd.at[iy], 1)
 
     def getting(k):
         return particles(k, dk.at[0], rd.at[lax.rem(iy + n_gy - k, n_gy)], 1)
 
-    for k in range(1, n_gy):
+    def gather_for(k, carry):
+        gather(lax.rem(iy + k, n_gy), carry)
         giving(k).start()
+        return carry
+
+    lax.fori_loop(1, n_gy, gather_for, 0)
+    gather(iy, 0)
     rd[iy] = dk[iy]
     for h in sent:
-        h.each("x", lambda c: c.wait_send())
-        h.each("y", lambda c: c.wait_send())
-        if h.corners:
-            h.each_corner(lambda c: c.wait_send())
+        for axis in "xyc":
+            h.each(axis, lambda c, _: c.wait_send())
     for k in range(1, n_gy):
         outgoing(k).wait_send()
         getting(k).wait_recv()
         giving(k).wait_send()
     for c in range(n_gy):
-        drag_out[c] = rd[c, 0:3, :]
+        for d in range(3):
+            drag_out[d, pl.ds(c, 1), :] = rd[c, d:d + 1, :]
 
 
 def solution(mesh):
@@ -391,7 +416,7 @@
             out_shape=(
                 jax.ShapeDtypeStruct(velocity.shape, F32),
                 jax.ShapeDtypeStruct(pressure.shape, F32),
-                jax.ShapeDtypeStruct((n_gy, 3, slots), F32),
+                jax.ShapeDtypeStruct((3, n_gy, slots), F32),
             ),
             in_specs=[pl.BlockSpec(memory_space=pltpu.SMEM)] + [vmem] * 5,
             out_specs=(vmem,) * 3,
@@ -404,8 +429,10 @@
                 pltpu.VMEM((n_gy, 3, slots), F32),
                 pltpu.VMEM((n_gy, 3, slots), F32),
                 pltpu.VMEM((4 * nz, 2 * bx * by), BF16),
-                pltpu.SemaphoreType.DMA((13, 8)),
-                pltpu.SemaphoreType.DMA((13, 8)),
+                pltpu.VMEM((14, 4, 16, nz), F32),
+                pltpu.VMEM((14, 4, 16, nz), F32),
+                pltpu.SemaphoreType.DMA((14, 8)),
+                pltpu.SemaphoreType.DMA((14, 8)),
                 pltpu.SemaphoreType.DMA((2, n_gy)),
                 pltpu.SemaphoreType.DMA((2, n_gy)),
             ],
@@ -417,10 +444,10 @@
             velocity,
             pressure,
             part_cell.reshape(n_gy, slots),
-            grain_velocities.reshape(n_gy, 3, slots),
+            grain_velocities.reshape(n_gy, 3, slots).transpose(1, 0, 2),
             part_vol.reshape(n_gy, slots),
         )
-        return v, p, drag.reshape(grain_velocities.shape)
+        return v, p, drag.transpose(1, 0, 2).reshape(grain_velocities.shape)
 
     placed = (
         P(None, "gx", "gy", None),

time: 76.5 us -> 60.6 us (0.79)
  Pallas kernels: 70.2 us -> 56.5 us
  local copies, waits for them, and re-layouts: 5.4 us -> 3.22 us
    pallas_call x1, Pallas kernels: 70.2 us -> 56.5 us  [per_device(): pl.pallas_call(kernel, name='interval', out_shape=(jax.ShapeDtypeStruct(v...]
    unnamed x6 -> x7, local copies, waits for them, and re-layouts: 5.4 us -> 3.22 us
where the time goes in v2:
time: 60.6 us; the launch traced here: 60.4 us
  Pallas kernels  56.5 us (93%)
  local copies, waits for them, and re-layouts  3.22 us (5%)
  between operations  0.65 us (1%)
    pallas_call x1, Pallas kernels, per_device(): pl.pallas_call(kernel, name='interval', out_shape=(jax.ShapeDtypeStruct(v...  56.5 us
    unnamed x7, local copies, waits for them, and re-layouts  3.22 us

profile of v2, /device:TPU:0, one launch (start us, length us, event | category | flops | bytes accessed | tf_op | source)
XLA Modules:
  0.0 60.4 jit_solution(6641399115495607053)
XLA Ops:
  0.6 56.5 %interval.1 = (f32[3,8,16,256]{3,2,1,0:T(8,128)}, f32[8,16,256]{2,1,0:T(8,128)}, f32[3,8,512]{2,1,0:T(8,128)}) custom-call(s32[8]{0:T(128)} %bitcast.13, f32[3,8,16,256]{3,2,1,0:T(8,128)} %refs_1_.1, f32[8,16,256]{2,1,0:T(8,128)} %refs_2_.1, s32[8,512]{1,0:T(8,128)} %bitcast.11, f32[3,8,512]{2,1,0:T(8,128)} %bitcast.10, f32[8,512]{1,0:T(8,128)} %bitcast.12), custom_call_target="tpu_custom_call" | custom-call | tf_op jit(solution)/shard_map/interval/pallas_call | solution.py:413
  57.2 0.0 copy-start
  57.2 1.8 %copy.12 = f32[3,8,16,256]{3,2,1,0:T(8,128)} copy(f32[3,8,16,256]{3,2,1,0:T(8,128)} %get-tuple-element.12) | data formatting | bytes 786432
  59.0 0.0 copy-done
  59.0 0.0 copy-start.1
  59.0 0.7 %copy.13 = f32[8,16,256]{2,1,0:T(8,128)} copy(f32[8,16,256]{2,1,0:T(8,128)S(1)} %copy-done) | data formatting | bytes 262144
  59.7 0.1 copy-done.1
  59.8 0.6 %copy.14 = f32[1,1,8,3,512]{4,2,3,1,0:T(8,128)} copy(f32[1,1,8,3,512]{4,2,3,1,0:T(8,128)S(1)} %bitcast.9) | data formatting | bytes 98304
Async XLA Ops:
  57.2 1.8 %copy-start = (f32[8,16,256]{2,1,0:T(8,128)S(1)}, f32[8,16,256]{2,1,0:T(8,128)}, u32[]{:S(2)}) copy-start(f32[8,16,256]{2,1,0:T(8,128)} %get-tuple-element.13) | copy-start | bytes 393220
  59.0 0.8 %copy-start.1 = (f32[3,8,512]{2,1,0:T(8,128)S(1)}, f32[3,8,512]{2,1,0:T(8,128)}, u32[]{:S(2)}) copy-start(f32[3,8,512]{2,1,0:T(8,128)} %get-tuple-element.8) | copy-start | bytes 147460

commit v3 on v2

--- a/solution.py
+++ b/solution.py
@@ -168,7 +168,7 @@
     def start(halos):
         for h in halos:
             h.pack()
-        for axis in "xcy":
+        for axis in "cxy":
             for h in halos:
                 h.each(axis, lambda c, _: c.start())
         sent.extend(halos)

time: 60.6 us -> 58.1 us (0.959)
  Pallas kernels: 56.5 us -> 54 us
    pallas_call x1, Pallas kernels: 56.5 us -> 54 us  [per_device(): pl.pallas_call(kernel, name='interval', out_shape=(jax.ShapeDtypeStruct(v...]
where the time goes in v3:
time: 58.1 us; the launch traced here: 57.9 us
  Pallas kernels  54 us (93%)
  local copies, waits for them, and re-layouts  3.22 us (6%)
  between operations  0.65 us (1%)
    pallas_call x1, Pallas kernels, per_device(): pl.pallas_call(kernel, name='interval', out_shape=(jax.ShapeDtypeStruct(v...  54 us
    unnamed x7, local copies, waits for them, and re-layouts  3.22 us

profile of v3, /device:TPU:0, one launch (start us, length us, event | category | flops | bytes accessed | tf_op | source)
XLA Modules:
  0.0 57.9 jit_solution(6846987903027714592)
XLA Ops:
  0.6 54.0 %interval.1 = (f32[3,8,16,256]{3,2,1,0:T(8,128)}, f32[8,16,256]{2,1,0:T(8,128)}, f32[3,8,512]{2,1,0:T(8,128)}) custom-call(s32[8]{0:T(128)} %bitcast.13, f32[3,8,16,256]{3,2,1,0:T(8,128)} %refs_1_.1, f32[8,16,256]{2,1,0:T(8,128)} %refs_2_.1, s32[8,512]{1,0:T(8,128)} %bitcast.11, f32[3,8,512]{2,1,0:T(8,128)} %bitcast.10, f32[8,512]{1,0:T(8,128)} %bitcast.12), custom_call_target="tpu_custom_call" | custom-call | tf_op jit(solution)/shard_map/interval/pallas_call | solution.py:413
  54.7 0.0 copy-start
  54.7 1.8 %copy.12 = f32[3,8,16,256]{3,2,1,0:T(8,128)} copy(f32[3,8,16,256]{3,2,1,0:T(8,128)} %get-tuple-element.12) | data formatting | bytes 786432
  56.5 0.0 copy-done
  56.5 0.0 copy-start.1
  56.5 0.7 %copy.13 = f32[8,16,256]{2,1,0:T(8,128)} copy(f32[8,16,256]{2,1,0:T(8,128)S(1)} %copy-done) | data formatting | bytes 262144
  57.1 0.1 copy-done.1
  57.3 0.6 %copy.14 = f32[1,1,8,3,512]{4,2,3,1,0:T(8,128)} copy(f32[1,1,8,3,512]{4,2,3,1,0:T(8,128)S(1)} %bitcast.9) | data formatting | bytes 98304
Async XLA Ops:
  54.7 1.8 %copy-start = (f32[8,16,256]{2,1,0:T(8,128)S(1)}, f32[8,16,256]{2,1,0:T(8,128)}, u32[]{:S(2)}) copy-start(f32[8,16,256]{2,1,0:T(8,128)} %get-tuple-element.13) | copy-start | bytes 393220
  56.5 0.8 %copy-start.1 = (f32[3,8,512]{2,1,0:T(8,128)S(1)}, f32[3,8,512]{2,1,0:T(8,128)}, u32[]{:S(2)}) copy-start(f32[3,8,512]{2,1,0:T(8,128)} %get-tuple-element.8) | copy-start | bytes 147460
